TPU v7x, 32 devices: a whole 2x2x4 slice. The times are simulated.
32 devices in a mesh: gx: 8 (over z, x), gy: 4 (over y, core).
Axes of the slice: x: 2, y: 2, z: 4, core: 2. Of those that a mesh axis runs over, the one named last changes fastest.
Arguments:
- features: bfloat16 [20, 32, 32, 1024], P(None, 'gx', 'gy'), may hold values from -6 to 6
- spectral_weight: float32 [2, 16, 16, 20, 20, 128], P(None, None, None, None, None, ('gx', 'gy')), may hold values from -5 to 5
- pointwise_weight: bfloat16 [20, 20], replicated, may hold values from -1.25 to 1.25
- pointwise_bias: float32 [20], replicated, may hold values from -3 to 3
- cotangent: bfloat16 [20, 32, 32, 1024], P(None, 'gx', 'gy'), may hold values from -21 to 21
Outputs:
- layer_output: bfloat16 [20, 32, 32, 1024], P(None, 'gx', 'gy')
- features_gradient: bfloat16 [20, 32, 32, 1024], P(None, 'gx', 'gy')
- spectral_gradient: float32 [2, 16, 16, 20, 20, 128], P(None, None, None, None, None, ('gx', 'gy'))
- pointwise_gradient: float32 [20, 20], replicated
- bias_gradient: float32 [20], replicated
All inputs are finite; a program needn't handle non-finite values.
Results may differ from a plain program's by a relative error of at most 0.0065.
Values sent between devices are 32-bit elements; how exact they have to be, the bound alone decides.
No kernel may reach another device: no remote copies, remote signals or barrier semaphores. Data moves between devices by JAX's collectives and lax.ppermute only.
A program may use at most 256 MiB of HBM per device.

v0:
```python
import math

import jax
import jax.numpy as jnp
from jax import lax
from jax.sharding import PartitionSpec as P

C = 20
MX = 16
MY = 16
MZ = 16
MT = 8
NZ = 64
NT = 16
MZT = 128


half_root = 0.7071067811865476
density_norm = 0.3989422804014327
highest = lax.Precision.HIGHEST


def kept_frequencies(length, mode_count):
    column = jnp.arange(mode_count, dtype=jnp.int32)
    return jnp.where(column < mode_count // 2, column, length - mode_count + column)


def complex_table(length, mode_count):
    phases = (
        kept_frequencies(length, mode_count)[:, None]
        * jnp.arange(length, dtype=jnp.int32)[None, :]
        % length
    )
    angles = 2.0 * math.pi / length * phases.astype(jnp.float32)
    scaling = 1.0 / math.sqrt(length)
    cosine_part = jnp.cos(angles) * scaling
    sine_part = -jnp.sin(angles) * scaling
    return jnp.stack([jnp.stack([cosine_part, -sine_part]), jnp.stack([sine_part, cosine_part])])


def make_depth_table():
    depth_phase = jnp.arange(NZ, dtype=jnp.int32)[:, None] * kept_frequencies(NZ, MZ)[None, :] % NZ
    time_phase = jnp.arange(NT, dtype=jnp.int32)[:, None] * kept_frequencies(NT, MT)[None, :] % NT
    phases = (depth_phase[:, None, :, None] * NT + time_phase[None, :, None, :] * NZ) % (NZ * NT)
    angles = 2.0 * math.pi / (NZ * NT) * phases.astype(jnp.float32)
    scaling = 1.0 / math.sqrt(NZ * NT)
    entries = jnp.stack([jnp.cos(angles) * scaling, -jnp.sin(angles) * scaling], axis=2)
    return entries.reshape(NZ * NT, 2, MZ * MT).astype(jnp.bfloat16)


def activation(hidden):
    cumulative = 0.5 * (1.0 + lax.erf(hidden * half_root))
    slopes = cumulative + hidden * density_norm * jnp.exp(-0.5 * hidden * hidden)
    return (hidden * cumulative, slopes)


def contract(form, weight_part, value_part):
    return jnp.einsum(form, weight_part, value_part, precision=highest)


def mix_forward(weights, values):
    form = "abcdm,cabm->dabm"
    real_out = contract(form, weights[0], values[0]) - contract(form, weights[1], values[1])
    imaginary = contract(form, weights[0], values[1]) + contract(form, weights[1], values[0])
    return jnp.stack([real_out, imaginary])


def mix_adjoint(weights, values):
    form = "abcdm,dabm->cabm"
    real_out = contract(form, weights[0], values[0]) + contract(form, weights[1], values[1])
    imaginary = contract(form, weights[0], values[1]) - contract(form, weights[1], values[0])
    return jnp.stack([real_out, imaginary])


def weight_gradient(back_values, values):
    form = "dabm,cabm->abcdm"
    real_out = contract(form, back_values[0], values[0]) + contract(form, back_values[1], values[1])
    imaginary = contract(form, back_values[1], values[0]) - contract(
        form, back_values[0], values[1]
    )
    return jnp.stack([real_out, imaginary])


def on_device(features, spectral_weight, pointwise_weight, pointwise_bias, cotangent):
    first_local = features.shape[1]
    second_local = features.shape[2]
    first_groups = lax.axis_size("gx")
    second_groups = lax.axis_size("gy")
    first_table = complex_table(first_local * first_groups, MX)
    second_table = complex_table(second_local * second_groups, MY)
    depth_rounded = make_depth_table()
    depth_float = lax.optimization_barrier(depth_rounded).astype(jnp.float32)
    first_grid_table = first_table.reshape(2, 2, MX, first_groups, first_local)
    second_grid_table = second_table.reshape(2, 2, MY, second_groups, second_local)

    def to_modes(cell_data):
        flattened = cell_data.reshape(2, C, first_local * second_local, MZT)
        arrived = lax.all_to_all(flattened, ("gx", "gy"), split_axis=3, concat_axis=2, tiled=True)
        blocks_grid = arrived.reshape(
            2, C, first_groups, second_groups, first_local, second_local, arrived.shape[3]
        )
        partly = jnp.einsum(
            "okagx,kcghxym->ocahym", first_grid_table, blocks_grid, precision=highest
        )
        return jnp.einsum("okbhy,kcahym->ocabm", second_grid_table, partly, precision=highest)

    def to_cells(values):
        partly = jnp.einsum("kobhy,kcabm->ocahym", second_grid_table, values, precision=highest)
        blocks_grid = jnp.einsum(
            "koagx,kcahym->ocghxym", first_grid_table, partly, precision=highest
        )
        flattened = blocks_grid.reshape(
            2, C, first_groups * second_groups * first_local * second_local, blocks_grid.shape[6]
        )
        returned = lax.all_to_all(flattened, ("gx", "gy"), split_axis=2, concat_axis=3, tiled=True)
        return returned.reshape(2, C, first_local, second_local, MZT)

    spectrum_cells = jnp.einsum(
        "cxys,skm->kcxym", features, depth_rounded, preferred_element_type=jnp.float32
    )
    spectrum = to_modes(spectrum_cells)
    mixed_modes = mix_forward(spectral_weight, spectrum)
    spectral = jnp.einsum("kcxym,skm->cxys", to_cells(mixed_modes), depth_float, precision=highest)
    pointwise = jnp.einsum(
        "ab,axys->bxys", pointwise_weight, features, preferred_element_type=jnp.float32
    )
    hidden = spectral + pointwise + pointwise_bias[:, None, None, None]
    activated, slopes = activation(hidden)
    layer_output = activated.astype(jnp.bfloat16)
    hidden_gradient = (cotangent.astype(jnp.float32) * slopes).astype(jnp.bfloat16)
    weight_terms = jnp.einsum(
        "axys,bxys->ab", features, hidden_gradient, preferred_element_type=jnp.float32
    )
    bias_terms = jnp.sum(hidden_gradient, axis=(1, 2, 3), dtype=jnp.float32)
    weight_total, bias_total = lax.psum((weight_terms, bias_terms), ("gx", "gy"))
    back_input = jnp.einsum(
        "cxys,skm->kcxym", hidden_gradient, depth_rounded, preferred_element_type=jnp.float32
    )
    back_spectrum = to_modes(back_input)
    spectral_gradient = weight_gradient(back_spectrum, spectrum)
    back_mixed = mix_adjoint(spectral_weight, back_spectrum)
    back_cells = jnp.einsum("kcxym,skm->cxys", to_cells(back_mixed), depth_float, precision=highest)
    back_pointwise = jnp.einsum(
        "ab,bxys->axys", pointwise_weight, hidden_gradient, preferred_element_type=jnp.float32
    )
    features_gradient = (back_cells + back_pointwise).astype(jnp.bfloat16)
    total_cells = first_local * first_groups * second_local * second_groups * NZ * NT
    scaling = 1.0 / math.sqrt(total_cells)
    return (
        layer_output,
        features_gradient,
        spectral_gradient,
        weight_total * scaling,
        bias_total * scaling,
    )


def solution(mesh):
    return jax.shard_map(
        on_device,
        mesh=mesh,
        in_specs=(
            P(None, "gx", "gy", None),
            P(None, None, None, None, None, ("gx", "gy")),
            P(),
            P(),
            P(None, "gx", "gy", None),
        ),
        out_specs=(
            P(None, "gx", "gy", None),
            P(None, "gx", "gy", None),
            P(None, None, None, None, None, ("gx", "gy")),
            P(),
            P(),
        ),
        check_vma=False,
    )
```

profile of v0, /device:TPU:0, one launch (start us, length us, event | category | flops | bytes accessed | tf_op | source)
XLA Modules:
  0.0 485.1 jit_solution(12313551475075560742)
XLA Ops:
  19.1 7.5 %all-to-all-start = ((f32[32,1,5120]{2,1,0:T(1,128)}), f32[32,1,5120]{2,1,0:T(1,128)S(1)}, u32[]{:S(2)}, u32[]{:S(2)}) async-start(f32[32,1,5120]{2,1,0:T(1,128)} %reshape.461), calls=%async_computation | async-start | bytes 1310720 | tf_op jit(solution)/shard_map/all_to_all | solution.py:98
  26.6 18.4 %slice_bitcast_fusion.1 = (f32[16,16,20,20,4]{3,4,2,1,0:T(4,128)}, f32[16,16,20,20,4]{3,4,2,1,0:T(4,128)}) fusion(f32[2,16,16,20,20,4]{4,5,3,2,1,0:T(4,128)} %param.6), kind=kLoop, calls=%fused_computation.4 | loop fusion | bytes 6553600 | tf_op jit(solution)/shard_map/squeeze | solution.py:63
  45.0 14.9 %copy.200 = f32[16,16,20,20,4]{2,3,4,1,0:T(8,128)} copy(f32[16,16,20,20,4]{3,4,2,1,0:T(4,128)} %get-tuple-element.35) | data formatting | bytes 3276800 | tf_op jit(solution)/shard_map/squeeze | solution.py:63
  59.9 14.9 %copy.197 = f32[16,16,20,20,4]{2,3,4,1,0:T(8,128)} copy(f32[16,16,20,20,4]{3,4,2,1,0:T(4,128)} %get-tuple-element.34) | data formatting | bytes 3276800 | tf_op jit(solution)/shard_map/squeeze | solution.py:63
  83.3 5.2 %copy.133 = f32[2,20,32,32,4]{1,3,4,2,0:T(8,128)} copy(f32[2,20,32,32,4]{3,4,2,1,0:T(4,128)} %bitcast.284) | data formatting | bytes 1310720 | tf_op jit(solution)/shard_map/all_to_all | solution.py:98
  88.5 6.9 %fusion.17 = f32[2,20,16,4,8,4,1]{1,2,0,5,4,3,6:T(8,128)S(1)} fusion(f32[2,20,8,4,4,8,4,1]{1,5,4,6,3,2,0,7:T(8,128)} %bitcast.272, f32[1,1,16,8,4]{2,3,4,1,0:T(8,128)S(1)} %copy-done.12, f32[1,1,16,8,4]{2,3,4,1,0:T(8,128)S(1)} %copy-done.10, f32[1,1,16,8,4]{2,3,4,1,0:T(8,128)S(1)} %copy-done.8), kind=kOutput, calls=%fused_computation.31 | convolution fusion | flops 62920704 | bytes 989184 | tf_op jit(solution)/shard_map/okagx,kcghxym->ocahym/dot_general | solution.py:102
  99.0 22.2 %fusion.74 = f32[16,16,4,1,20]{4,3,2,1,0:T(1,128)S(1)} fusion(f32[16,16,20,20,4]{2,3,4,1,0:T(8,128)} %copy.200, f32[20,16,16,4,1]{0,2,3,1,4:T(8,128)S(1)} %get-tuple-element.40), kind=kOutput, calls=%fused_computation.98 | convolution fusion | flops 4915200 | bytes 1802240 | tf_op jit(solution)/shard_map/abcdm,cabm->dabm/dot_general | solution.py:58
  121.2 19.7 %fusion.72 = f32[16,16,4,1,20]{4,3,2,1,0:T(1,128)S(1)} fusion(f32[16,16,20,20,4]{2,3,4,1,0:T(8,128)S(1)} %bitcast.265, f32[20,16,16,4,1]{0,2,3,1,4:T(8,128)S(1)} %get-tuple-element.41), kind=kOutput, calls=%fused_computation.96 | convolution fusion | flops 4915200 | bytes 1802240 | tf_op jit(solution)/shard_map/abcdm,cabm->dabm/dot_general | solution.py:58
  141.0 20.1 %fusion.70 = f32[16,16,4,1,20]{4,3,2,1,0:T(1,128)S(1)} fusion(f32[16,16,20,20,4]{2,3,4,1,0:T(8,128)S(1)} %bitcast.269, f32[20,16,16,4,1]{0,2,3,1,4:T(8,128)S(1)} %get-tuple-element.41), kind=kOutput, calls=%fused_computation.94 | convolution fusion | flops 4915200 | bytes 1802240 | tf_op jit(solution)/shard_map/abcdm,cabm->dabm/dot_general | solution.py:58
  161.2 20.1 %fusion.76 = f32[16,16,4,1,20]{4,3,2,1,0:T(1,128)S(1)} fusion(f32[16,16,20,20,4]{2,3,4,1,0:T(8,128)S(1)} %bitcast.269, f32[20,16,16,4,1]{0,2,3,1,4:T(8,128)S(1)} %get-tuple-element.40), kind=kOutput, calls=%fused_computation.100 | convolution fusion | flops 4915200 | bytes 1802240 | tf_op jit(solution)/shard_map/abcdm,cabm->dabm/dot_general | solution.py:58
  183.3 5.3 %convolution_bitcast_fusion.1 = f32[2,20,8,4,4,8,4]{1,2,4,0,6,5,3:T(8,128)S(1)} fusion(f32[2,20,16,4,8,4,1,1]{1,4,3,0,5,2,7,6:T(8,128)S(1)} %convolution_bitcast_fusion.3, f32[1,1,16,8,4]{2,3,4,1,0:T(8,128)S(1)} %copy-done.12, f32[1,1,16,8,4]{2,3,4,1,0:T(8,128)S(1)} %copy-done.10, f32[1,1,16,8,4]{2,3,4,1,0:T(8,128)S(1)} %copy-done.8), kind=kOutput, calls=%fused_computation.23 | convolution fusion | flops 62920704 | bytes 989184 | tf_op jit(solution)/shard_map/koagx,kcahym->ocghxym/dot_general | solution.py:109
  191.0 5.0 %copy.311 = f32[2,20,1024,4]{1,3,0,2:T(4,128)} copy(f32[2,20,1024,4]{1,2,3,0:T(8,128)S(1)} %bitcast.273) | data formatting | bytes 1310720 | tf_op jit(solution)/shard_map/reshape | solution.py:112
  196.1 7.3 %reshape.463 = f32[32,1,5120]{2,1,0:T(1,128)} reshape(f32[1024,2,4,20]{3,2,1,0:T(4,128)} %bitcast.274) | data formatting | bytes 1310720
  203.4 6.1 %all-to-all-start.1 = ((f32[32,1,5120]{2,1,0:T(1,128)}), f32[32,1,5120]{2,1,0:T(1,128)}, u32[]{:S(2)}, u32[]{:S(2)}) async-start(f32[32,1,5120]{2,1,0:T(1,128)} %reshape.463), calls=%async_computation.1 | async-start | bytes 1310720 | tf_op jit(solution)/shard_map/all_to_all | solution.py:115
  212.9 14.5 %all-to-all-done.1 = f32[32,1,5120]{2,1,0:T(1,128)} async-done(((f32[32,1,5120]{2,1,0:T(1,128)}), f32[32,1,5120]{2,1,0:T(1,128)}, u32[]{:S(2)}, u32[]{:S(2)}) %all-to-all-start.1) | async-done | bytes 655392 | tf_op jit(solution)/shard_map/all_to_all | solution.py:115
  231.5 8.2 %reshape.464 = f32[1024,2,4,20]{3,2,1,0:T(4,128)} reshape(f32[32,5120]{1,0:T(8,128)} %reduce.1) | data formatting | bytes 1310720
  239.8 5.0 %copy.141 = f32[2,20,32,32,4]{1,3,4,2,0:T(8,128)} copy(f32[2,20,32,32,4]{1,4,0,3,2:T(4,128)} %bitcast.275) | data formatting | bytes 1310720 | tf_op jit(solution)/shard_map/all_to_all | solution.py:115
  248.9 6.5 %convert_reduce_fusion = (f32[20]{0:T(128)S(1)}, bf16[20,4,8,1024]{3,2,1,0:T(8,128)(2,1)S(1)}, bf16[20,4,8,1024]{3,2,1,0:T(8,128)(2,1)}) fusion(bf16[20,4,8,1024]{3,2,1,0:T(8,128)(2,1)} %param.9, f32[20]{0:T(128)S(1)} %copy-done.20, f32[20,4,8,1024]{3,0,2,1:T(8,128)S(1)} %fusion.33, f32[2,20,4,8,128]{4,3,0,2,1:T(8,128)} %copy.142, ...), kind=kOutput, calls=%fused_computation.19 | convolution fusion | flops 2024407040 | bytes 7733408 | tf_op jit(solution)/shard_map/kcxym,skm->cxys/dot_general | solution.py:123
  279.0 40.8 %all-reduce = (f32[20,20]{0,1:T(8,128)S(1)}, f32[20]{0:T(128)S(1)}) all-reduce(f32[20,20]{0,1:T(8,128)S(1)} %fusion.42, f32[20]{0:T(128)S(1)} %get-tuple-element.32), channel_id=1, replica_groups=mesh['gx'=8,'gy'=4] {'gx','gy'}, use_global_device_ids=true, to_apply=%region_0.1 | all-reduce | flops 420 | bytes 3360 | tf_op jit(solution)/shard_map/psum | solution.py:135
  337.3 5.2 %copy.149 = f32[2,20,32,32,4]{1,3,4,2,0:T(8,128)} copy(f32[2,20,32,32,4]{3,4,2,1,0:T(4,128)} %bitcast.287) | data formatting | bytes 1310720 | tf_op jit(solution)/shard_map/all_to_all | solution.py:98
  342.5 6.9 %fusion.20 = f32[2,20,16,4,8,4,1]{1,2,0,5,4,3,6:T(8,128)S(1)} fusion(f32[2,20,8,4,4,8,4,1]{1,5,4,6,3,2,0,7:T(8,128)} %bitcast.277, f32[1,1,16,8,4]{2,3,4,1,0:T(8,128)S(1)} %copy-done.13, f32[1,1,16,8,4]{2,3,4,1,0:T(8,128)S(1)} %copy-done.11, f32[1,1,16,8,4]{2,3,4,1,0:T(8,128)S(1)} %copy-done.9), kind=kOutput, calls=%fused_computation.32 | convolution fusion | flops 62920704 | bytes 989184 | tf_op jit(solution)/shard_map/okagx,kcghxym->ocahym/dot_general | solution.py:102
  353.0 14.5 %fusion.62 = f32[16,16,4,1,20]{4,3,2,1,0:T(1,128)S(1)} fusion(f32[16,16,20,20,4]{2,3,4,1,0:T(8,128)} %copy.197, f32[20,16,16,4,1]{0,2,3,1,4:T(8,128)S(1)} %get-tuple-element.45), kind=kOutput, calls=%fused_computation.86 | convolution fusion | flops 4915200 | bytes 1802240 | tf_op jit(solution)/shard_map/abcdm,dabm->cabm/dot_general | solution.py:58
  367.5 12.0 %fusion.64 = f32[16,16,4,1,20]{4,3,2,1,0:T(1,128)S(1)} fusion(f32[16,16,20,20,4]{2,3,4,1,0:T(8,128)S(1)} %bitcast.267, f32[20,16,16,4,1]{0,2,3,1,4:T(8,128)S(1)} %get-tuple-element.45), kind=kOutput, calls=%fused_computation.88 | convolution fusion | flops 4915200 | bytes 1802240 | tf_op jit(solution)/shard_map/abcdm,dabm->cabm/dot_general | solution.py:58
  379.6 12.2 %fusion.66 = f32[16,16,4,1,20]{4,3,2,1,0:T(1,128)S(1)} fusion(f32[16,16,20,20,4]{2,3,4,1,0:T(8,128)S(1)} %bitcast.267, f32[20,16,16,4,1]{0,2,3,1,4:T(8,128)S(1)} %get-tuple-element.44), kind=kOutput, calls=%fused_computation.90 | convolution fusion | flops 4915200 | bytes 1802240 | tf_op jit(solution)/shard_map/abcdm,dabm->cabm/dot_general | solution.py:58
  391.8 12.4 %fusion.68 = f32[16,16,4,1,20]{4,3,2,1,0:T(1,128)S(1)} fusion(f32[16,16,20,20,4]{2,3,4,1,0:T(8,128)S(1)} %bitcast.271, f32[20,16,16,4,1]{0,2,3,1,4:T(8,128)S(1)} %get-tuple-element.44), kind=kOutput, calls=%fused_computation.92 | convolution fusion | flops 4915200 | bytes 1802240 | tf_op jit(solution)/shard_map/abcdm,dabm->cabm/dot_general | solution.py:58
  406.2 5.3 %convolution_bitcast_fusion = f32[2,20,8,4,4,8,4]{1,2,4,0,6,5,3:T(8,128)S(1)} fusion(f32[2,20,16,4,8,4,1,1]{1,4,3,0,5,2,7,6:T(8,128)S(1)} %convolution_bitcast_fusion.2, f32[1,1,16,8,4]{2,3,4,1,0:T(8,128)S(1)} %copy-done.13, f32[1,1,16,8,4]{2,3,4,1,0:T(8,128)S(1)} %copy-done.11, f32[1,1,16,8,4]{2,3,4,1,0:T(8,128)S(1)} %copy-done.9), kind=kOutput, calls=%fused_computation.22 | convolution fusion | flops 62920704 | bytes 989184 | tf_op jit(solution)/shard_map/koagx,kcahym->ocghxym/dot_general | solution.py:109
  418.8 7.3 %reshape.467 = f32[32,1,5120]{2,1,0:T(1,128)} reshape(f32[1024,2,4,20]{3,2,1,0:T(4,128)} %bitcast.279) | data formatting | bytes 1310720
  434.7 15.2 %add_bitcast_fusion = (f32[1,16,16,20,20,4]{4,5,3,2,1,0:T(4,128)S(1)}, f32[1,16,16,20,20,4]{4,5,3,2,1,0:T(4,128)S(1)}) fusion(f32[16,16,4,20]{3,2,1,0:T(4,128)} %copy.164, f32[16,16,4,20]{2,3,1,0:T(8,128)S(1)} %copy.163, f32[16,16,4,20]{3,2,1,0:T(4,128)} %copy.162, f32[16,16,4,20]{2,3,1,0:T(8,128)} %copy.161), kind=kLoop, calls=%fused_computation.2 | loop fusion | flops 2457600 | bytes 3604480 | tf_op jit(solution)/shard_map/stack | solution.py:81
  449.9 10.0 %pad_maximum_fusion = f32[2,16,16,20,20,4]{4,5,3,2,1,0:T(4,128)} fusion(f32[1,16,16,20,20,4]{4,5,3,2,1,0:T(4,128)S(1)} %get-tuple-element.37, f32[1,16,16,20,20,4]{4,5,3,2,1,0:T(4,128)S(1)} %get-tuple-element.36), kind=kLoop, calls=%fused_computation | loop fusion | flops 819200 | bytes 6553600 | tf_op jit(solution)/shard_map/stack | solution.py:81
  463.3 7.3 %reshape.468 = f32[1024,2,4,20]{3,2,1,0:T(4,128)} reshape(f32[32,5120]{1,0:T(8,128)S(1)} %reduce.3) | data formatting | bytes 1310720
  470.6 5.0 %copy.157 = f32[2,20,32,32,4]{1,3,4,2,0:T(8,128)} copy(f32[2,20,32,32,4]{1,4,0,3,2:T(4,128)} %bitcast.280) | data formatting | bytes 1310720 | tf_op jit(solution)/shard_map/all_to_all | solution.py:115
  479.9 5.0 %fusion.9 = bf16[20,4,8,1024]{3,2,1,0:T(8,128)(2,1)} fusion(f32[4,8,1024,20]{2,3,1,0:T(8,128)S(1)} %copy-done.2, f32[2,20,4,8,128]{4,3,0,2,1:T(8,128)} %copy.158, bf16[1024,2,128]{2,0,1:T(8,128)(2,1)} %pad_maximum_fusion.1), kind=kOutput, calls=%fused_computation.16 | convolution fusion | flops 2014576640 | bytes 5111808 | tf_op jit(solution)/shard_map/kcxym,skm->cxys/dot_general | solution.py:142
  (128 shorter events, 116.8 us)
Async XLA Ops:
  0.6 209.7 %copy-start = (bf16[20,20]{1,0:T(8,128)(2,1)S(1)}, bf16[20,20]{1,0:T(8,128)(2,1)}, u32[]{:S(2)}) copy-start(bf16[20,20]{1,0:T(8,128)(2,1)} %param.7) | copy-start | bytes 2404
  3.4 7.2 %copy-start.3 = (bf16[20,4,8,1024]{3,2,1,0:T(8,128)(2,1)S(1)}, bf16[20,4,8,1024]{3,2,1,0:T(8,128)(2,1)}, u32[]{:S(2)}) copy-start(bf16[20,4,8,1024]{3,2,1,0:T(8,128)(2,1)} %param.5) | copy-start | bytes 3932164
  19.1 57.3 %all-to-all-start = ((f32[32,1,5120]{2,1,0:T(1,128)}), f32[32,1,5120]{2,1,0:T(1,128)S(1)}, u32[]{:S(2)}, u32[]{:S(2)}) async-start(f32[32,1,5120]{2,1,0:T(1,128)} %reshape.461), calls=%async_computation | async-start | bytes 1310720 | tf_op jit(solution)/shard_map/all_to_all | solution.py:98
  83.3 5.2 %copy-start.8 = (f32[1,1,16,8,4]{2,3,4,1,0:T(8,128)S(1)}, f32[1,1,16,8,4]{2,3,4,1,0:T(8,128)}, u32[]{:S(2)}) copy-start(f32[1,1,16,8,4]{2,3,4,1,0:T(8,128)} %get-tuple-element.52) | copy-start | bytes 6148
  83.3 5.2 %copy-start.10 = (f32[1,1,16,8,4]{2,3,4,1,0:T(8,128)S(1)}, f32[1,1,16,8,4]{2,3,4,1,0:T(8,128)}, u32[]{:S(2)}) copy-start(f32[1,1,16,8,4]{2,3,4,1,0:T(8,128)} %get-tuple-element.53) | copy-start | bytes 6148
  83.3 5.2 %copy-start.12 = (f32[1,1,16,8,4]{2,3,4,1,0:T(8,128)S(1)}, f32[1,1,16,8,4]{2,3,4,1,0:T(8,128)}, u32[]{:S(2)}) copy-start(f32[1,1,16,8,4]{2,3,4,1,0:T(8,128)} %get-tuple-element.54) | copy-start | bytes 6148
  88.5 7.0 %copy-start.14 = (f32[1,1,16,4,8]{2,4,1,3,0:T(8,128)S(1)}, f32[1,1,16,4,8]{2,4,1,3,0:T(8,128)}, u32[]{:S(2)}) copy-start(f32[1,1,16,4,8]{2,4,1,3,0:T(8,128)} %get-tuple-element.49) | copy-start | bytes 6148
  88.5 7.0 %copy-start.16 = (f32[1,1,16,4,8]{2,4,1,3,0:T(8,128)S(1)}, f32[1,1,16,4,8]{2,4,1,3,0:T(8,128)}, u32[]{:S(2)}) copy-start(f32[1,1,16,4,8]{2,4,1,3,0:T(8,128)} %get-tuple-element.50) | copy-start | bytes 6148
  88.5 7.0 %copy-start.18 = (f32[1,1,16,4,8]{2,4,1,3,0:T(8,128)S(1)}, f32[1,1,16,4,8]{2,4,1,3,0:T(8,128)}, u32[]{:S(2)}) copy-start(f32[1,1,16,4,8]{2,4,1,3,0:T(8,128)} %get-tuple-element.51) | copy-start | bytes 6148
  95.5 25.7 %slice-start = ((s8[12582912]{0:T(1024)(128)(4,1)}), s8[4194304]{0:T(1024)(128)(4,1)S(1)}, s32[]{:S(2)}) async-start(s8[12582912]{0:T(1024)(128)(4,1)} %bitcast.264), calls=%async_computation.4 | async-start | bytes 8388608
  99.0 22.2 %slice-start.1 = ((s8[12582912]{0:T(1024)(128)(4,1)}), s8[4194304]{0:T(1024)(128)(4,1)S(1)}, s32[]{:S(2)}) async-start(s8[12582912]{0:T(1024)(128)(4,1)} %bitcast.264), calls=%async_computation.5 | async-start | bytes 8388608
  99.0 22.2 %slice-start.2 = ((s8[12582912]{0:T(1024)(128)(4,1)}), s8[4194304]{0:T(1024)(128)(4,1)S(1)}, s32[]{:S(2)}) async-start(s8[12582912]{0:T(1024)(128)(4,1)} %bitcast.264), calls=%async_computation.6 | async-start | bytes 8388608
  99.0 42.0 %slice-start.6 = ((s8[12582912]{0:T(1024)(128)(4,1)}), s8[4194304]{0:T(1024)(128)(4,1)S(1)}, s32[]{:S(2)}) async-start(s8[12582912]{0:T(1024)(128)(4,1)} %bitcast.268), calls=%async_computation.10 | async-start | bytes 8388608
  99.0 42.0 %slice-start.7 = ((s8[12582912]{0:T(1024)(128)(4,1)}), s8[4194304]{0:T(1024)(128)(4,1)S(1)}, s32[]{:S(2)}) async-start(s8[12582912]{0:T(1024)(128)(4,1)} %bitcast.268), calls=%async_computation.11 | async-start | bytes 8388608
  121.2 19.8 %slice-start.8 = ((s8[12582912]{0:T(1024)(128)(4,1)}), s8[4194304]{0:T(1024)(128)(4,1)S(1)}, s32[]{:S(2)}) async-start(s8[12582912]{0:T(1024)(128)(4,1)} %bitcast.268), calls=%async_computation.12 | async-start | bytes 8388608
  196.1 13.4 %copy-start.6 = (bf16[1024,1,128]{2,0,1:T(8,128)(2,1)S(1)}, bf16[1024,1,128]{2,0,1:T(8,128)(2,1)}, u32[]{:S(2)}) copy-start(bf16[1024,1,128]{2,0,1:T(8,128)(2,1)} %copy-done.5) | copy-start | bytes 786436
  203.4 24.0 %all-to-all-start.1 = ((f32[32,1,5120]{2,1,0:T(1,128)}), f32[32,1,5120]{2,1,0:T(1,128)}, u32[]{:S(2)}, u32[]{:S(2)}) async-start(f32[32,1,5120]{2,1,0:T(1,128)} %reshape.463), calls=%async_computation.1 | async-start | bytes 1310720 | tf_op jit(solution)/shard_map/all_to_all | solution.py:115
  248.9 6.5 %copy-start.7 = (bf16[1024,1,128]{2,0,1:T(8,128)(2,1)S(1)}, bf16[1024,1,128]{2,0,1:T(8,128)(2,1)}, u32[]{:S(2)}) copy-start(bf16[1024,1,128]{2,0,1:T(8,128)(2,1)} %copy-done.5) | copy-start | bytes 786436
  264.0 61.0 %all-to-all-start.2 = ((f32[32,1,5120]{2,1,0:T(1,128)}), f32[32,1,5120]{2,1,0:T(1,128)}, u32[]{:S(2)}, u32[]{:S(2)}) async-start(f32[32,1,5120]{2,1,0:T(1,128)} %reshape.465), calls=%async_computation.2 | async-start | bytes 1310720 | tf_op jit(solution)/shard_map/all_to_all | solution.py:98
  337.3 5.2 %copy-start.11 = (f32[1,1,16,8,4]{2,3,4,1,0:T(8,128)S(1)}, f32[1,1,16,8,4]{2,3,4,1,0:T(8,128)}, u32[]{:S(2)}) copy-start(f32[1,1,16,8,4]{2,3,4,1,0:T(8,128)} %get-tuple-element.53) | copy-start | bytes 6148
  337.3 5.2 %copy-start.13 = (f32[1,1,16,8,4]{2,3,4,1,0:T(8,128)S(1)}, f32[1,1,16,8,4]{2,3,4,1,0:T(8,128)}, u32[]{:S(2)}) copy-start(f32[1,1,16,8,4]{2,3,4,1,0:T(8,128)} %get-tuple-element.54) | copy-start | bytes 6148
  342.4 7.0 %copy-start.15 = (f32[1,1,16,4,8]{2,4,1,3,0:T(8,128)S(1)}, f32[1,1,16,4,8]{2,4,1,3,0:T(8,128)}, u32[]{:S(2)}) copy-start(f32[1,1,16,4,8]{2,4,1,3,0:T(8,128)} %get-tuple-element.49) | copy-start | bytes 6148
  342.4 7.0 %copy-start.17 = (f32[1,1,16,4,8]{2,4,1,3,0:T(8,128)S(1)}, f32[1,1,16,4,8]{2,4,1,3,0:T(8,128)}, u32[]{:S(2)}) copy-start(f32[1,1,16,4,8]{2,4,1,3,0:T(8,128)} %get-tuple-element.50) | copy-start | bytes 6148
  342.4 7.0 %copy-start.19 = (f32[1,1,16,4,8]{2,4,1,3,0:T(8,128)S(1)}, f32[1,1,16,4,8]{2,4,1,3,0:T(8,128)}, u32[]{:S(2)}) copy-start(f32[1,1,16,4,8]{2,4,1,3,0:T(8,128)} %get-tuple-element.51) | copy-start | bytes 6148
  349.4 18.1 %slice-start.3 = ((s8[12582912]{0:T(1024)(128)(4,1)}), s8[4194304]{0:T(1024)(128)(4,1)S(1)}, s32[]{:S(2)}) async-start(s8[12582912]{0:T(1024)(128)(4,1)} %bitcast.266), calls=%async_computation.7 | async-start | bytes 8388608
  353.0 14.5 %slice-start.4 = ((s8[12582912]{0:T(1024)(128)(4,1)}), s8[4194304]{0:T(1024)(128)(4,1)S(1)}, s32[]{:S(2)}) async-start(s8[12582912]{0:T(1024)(128)(4,1)} %bitcast.266), calls=%async_computation.8 | async-start | bytes 8388608
  353.0 14.5 %slice-start.5 = ((s8[12582912]{0:T(1024)(128)(4,1)}), s8[4194304]{0:T(1024)(128)(4,1)S(1)}, s32[]{:S(2)}) async-start(s8[12582912]{0:T(1024)(128)(4,1)} %bitcast.266), calls=%async_computation.9 | async-start | bytes 8388608
  367.5 24.2 %slice-start.9 = ((s8[12582912]{0:T(1024)(128)(4,1)}), s8[4194304]{0:T(1024)(128)(4,1)S(1)}, s32[]{:S(2)}) async-start(s8[12582912]{0:T(1024)(128)(4,1)} %bitcast.270), calls=%async_computation.13 | async-start | bytes 8388608
  367.5 24.2 %slice-start.10 = ((s8[12582912]{0:T(1024)(128)(4,1)}), s8[4194304]{0:T(1024)(128)(4,1)S(1)}, s32[]{:S(2)}) async-start(s8[12582912]{0:T(1024)(128)(4,1)} %bitcast.270), calls=%async_computation.14 | async-start | bytes 8388608
  379.5 12.2 %slice-start.11 = ((s8[12582912]{0:T(1024)(128)(4,1)}), s8[4194304]{0:T(1024)(128)(4,1)S(1)}, s32[]{:S(2)}) async-start(s8[12582912]{0:T(1024)(128)(4,1)} %bitcast.270), calls=%async_computation.15 | async-start | bytes 8388608
  426.0 33.9 %all-to-all-start.3 = ((f32[32,1,5120]{2,1,0:T(1,128)}), f32[32,1,5120]{2,1,0:T(1,128)}, u32[]{:S(2)}, u32[]{:S(2)}) async-start(f32[32,1,5120]{2,1,0:T(1,128)} %reshape.467), calls=%async_computation.3 | async-start | bytes 1310720 | tf_op jit(solution)/shard_map/all_to_all | solution.py:115
  475.6 9.3 %copy-start.1 = (bf16[20,20]{1,0:T(8,128)(2,1)S(1)}, bf16[20,20]{1,0:T(8,128)(2,1)}, u32[]{:S(2)}) copy-start(bf16[20,20]{1,0:T(8,128)(2,1)} %param.7) | copy-start | bytes 2404
  (5 other events, 17.2 us)
where the time goes:
time: 492 us; the launch traced here: 485 us
  matrix products  192 us (39%)
  local copies, waits for them, and re-layouts  167 us (34%)
  other arithmetic  47.1 us (10%)
  blocking collectives  40.8 us (8%)
  starting transfers between devices  21.7 us (4%)
  waiting for transfers between devices  14.5 us (3%)
    dot_general x8, matrix products, contract(): return jnp.einsum(form, weight_part, value_part, precision=highest)  133 us
    unnamed x75, local copies, waits for them, and re-layouts  44.3 us
    psum x1, blocking collectives, on_device(): lax.psum((weight_terms, bias_terms), ('gx', 'gy'))  40.8 us
    squeeze x2, local copies, waits for them, and re-layouts, mix_forward(): weights[0]  33.4 us
    another operation x2, other arithmetic, weight_gradient(): return jnp.stack([real_out, imaginary])  25.2 us
    all_to_all x5, local copies, waits for them, and re-layouts, to_modes(): lax.all_to_all(flattened, ('gx', 'gy'), split_axis=3, concat_axis=2, tile...  16.6 us
    squeeze x1, local copies, waits for them, and re-layouts, mix_forward(): weights[1]  14.9 us
    all_to_all x2, waiting for transfers between devices, to_cells(): lax.all_to_all(flattened, ('gx', 'gy'), split_axis=2, concat_axis=3, tile...  14.5 us
  transfers between devices with their start and end apart: 4, of which 1 were waited for; matrix products, arithmetic and copies ran while one was open for 20% of the time, Pallas kernels for 0%

commit v1 on v0

--- a/solution.py
+++ b/solution.py
@@ -1,8 +1,12 @@
+import functools
 import math
 
 import jax
 import jax.numpy as jnp
+import numpy as np
 from jax import lax
+from jax.experimental import pallas as pl
+from jax.experimental.pallas import tpu as pltpu
 from jax.sharding import PartitionSpec as P
 
 C = 20
@@ -13,11 +17,504 @@
 NZ = 64
 NT = 16
 MZT = 128
+ZT = NZ * NT
+AB = MX * MY
+CP = 24
+PAIRS = C * 4
+BLOCK = 256
 
 
 half_root = 0.7071067811865476
 density_norm = 0.3989422804014327
 highest = lax.Precision.HIGHEST
+f32 = jnp.float32
+bf16 = jnp.bfloat16
+
+
+def frequencies(length, mode_count):
+    column = np.arange(mode_count)
+    return np.where(column < mode_count // 2, column, length - mode_count + column)
+
+
+def depth_rows(devices):
+    kz = frequencies(NZ, MZ)
+    kt = frequencies(NT, MT)
+    z = np.arange(NZ)
+    t = np.arange(NT)
+    phase = (
+        (kz[:, None, None, None] * z[None, None, :, None] * NT)
+        + (kt[None, :, None, None] * t[None, None, None, :] * NZ)
+    ) % ZT
+    angle = 2.0 * np.pi / ZT * phase.reshape(MZT, ZT)
+    parts = np.stack([np.cos(angle), -np.sin(angle)]) / math.sqrt(ZT)
+    local = MZT // devices
+    rows = parts.reshape(2, devices, local, ZT).transpose(1, 0, 2, 3)
+    return rows.reshape(2 * MZT, ZT).astype(np.float32)
+
+
+def plane_table(first_groups, second_groups, first_local, second_local):
+    nx = first_groups * first_local
+    ny = second_groups * second_local
+    kx = frequencies(nx, MX)
+    ky = frequencies(ny, MY)
+    gx, gy, cx, cy = np.meshgrid(
+        np.arange(first_groups),
+        np.arange(second_groups),
+        np.arange(first_local),
+        np.arange(second_local),
+        indexing="ij",
+    )
+    x = (gx * first_local + cx).reshape(-1)
+    y = (gy * second_local + cy).reshape(-1)
+    ax = 2.0 * np.pi / nx * (kx[:, None] * x[None, :] % nx)
+    ay = 2.0 * np.pi / ny * (ky[:, None] * y[None, :] % ny)
+    angle = (ax[:, None, :] + ay[None, :, :]).reshape(AB, nx * ny)
+    return np.concatenate([np.cos(angle), np.sin(angle)]) / math.sqrt(nx * ny)
+
+
+def split(values):
+    high = values.astype(bf16)
+    return high, (values - high.astype(f32)).astype(bf16)
+
+
+def dot(left, right, dims):
+    return lax.dot_general(left, right, (dims, ((), ())), preferred_element_type=f32)
+
+
+NN = ((1,), (0,))
+NT_DIMS = ((1,), (1,))
+TN = ((0,), (0,))
+
+
+def compiler(limit=None):
+    return pltpu.CompilerParams(vmem_limit_bytes=limit or 60 * 1024 * 1024)
+
+
+def whole(memory=pltpu.VMEM):
+    return pl.BlockSpec(memory_space=memory)
+
+
+def depth_kernel(table_ref, cells_ref, out_ref):
+    out = dot(table_ref[...], cells_ref[...], NT_DIMS)
+    out_ref[...] = out.reshape(out_ref.shape)
+
+
+def swap_blocks(tiles):
+    lane = lax.broadcasted_iota(jnp.int32, tiles[0].shape, tiles[0].ndim - 1)
+    axis = tiles[0].ndim - 1
+    low = lane < 64
+    even = (lane // 32) % 2 == 0
+    t0, t1, t2, t3 = tiles
+
+    def far(u, v):
+        return jnp.where(low, u, pltpu.roll(v, 64, axis)), jnp.where(low, pltpu.roll(u, 64, axis), v)
+
+    def near(u, v):
+        return jnp.where(even, u, pltpu.roll(v, 32, axis)), jnp.where(even, pltpu.roll(u, 96, axis), v)
+
+    a0, a2 = far(t0, t2)
+    a1, a3 = far(t1, t3)
+    b0, b1 = near(a0, a1)
+    b2, b3 = near(a2, a3)
+    return b0, b1, b2, b3
+
+
+def row_sign(shape, top):
+    row = lax.broadcasted_iota(jnp.int32, shape, len(shape) - 2)
+    return jnp.where(row % 8 < 4, top, -top).astype(f32)
+
+
+def to_plane_modes(recv_ref, high_ref, low_ref, cells_ref, modes_ref):
+    for group in range(C // 4):
+        lanes = pl.ds(group * 128, 128)
+        tiles = [recv_ref[:, j, :, lanes] for j in range(4)]
+        for i, tile in enumerate(swap_blocks(tiles)):
+            for s in range(tile.shape[0]):
+                cells_ref[pl.ds((group * 4 + i) * 8, 8), pl.ds(s * 128, 128)] = tile[s]
+    high, low = split(cells_ref[...])
+    out = (
+        dot(high, high_ref[...], NT_DIMS)
+        + dot(high, low_ref[...], NT_DIMS)
+        + dot(low, high_ref[...], NT_DIMS)
+    )
+    cosine = out[:, :AB].reshape(C, 8, AB)
+    sine = out[:, AB:].reshape(C, 8, AB)
+    modes_ref[...] = cosine + row_sign(sine.shape, 1.0) * pltpu.roll(sine, 4, 1)
+
+
+def to_plane_cells(mixed, high_ref, low_ref, cells_ref, out_ref):
+    high, low = split(mixed)
+
+    def product(rows):
+        return (
+            dot(high, high_ref[rows, :], NN)
+            + dot(high, low_ref[rows, :], NN)
+            + dot(low, high_ref[rows, :], NN)
+        ).reshape(C, 8, high_ref.shape[1])
+
+    cosine = product(pl.ds(0, AB))
+    sine = product(pl.ds(AB, AB))
+    cells_ref[...] = (
+        cosine + row_sign(sine.shape, -1.0) * pltpu.roll(sine, 4, 1)
+    ).reshape(cells_ref.shape)
+    groups = out_ref.shape[0]
+    for group in range(C // 4):
+        tiles = [
+            jnp.stack(
+                [
+                    cells_ref[pl.ds((group * 4 + i) * 8, 8), pl.ds(s * 128, 128)]
+                    for s in range(groups)
+                ]
+            )
+            for i in range(4)
+        ]
+        for j, tile in enumerate(swap_blocks(tiles)):
+            out_ref[:, j, :, pl.ds(group * 128, 128)] = tile
+
+
+def weight_kernel(weight_ref, out_ref, wide_ref):
+    wide_ref[:, pl.ds(0, C)] = weight_ref[0, 0]
+    row = lax.broadcasted_iota(jnp.int32, (CP, 128), 0)
+
+    def step(pair, carry):
+        rows = wide_ref[pl.ds(pair, 128, stride=PAIRS), :]
+        out_ref[0, 0, pair] = jnp.where(row < C, rows.T[:CP], 0.0)
+        return carry
+
+    lax.fori_loop(0, PAIRS, step, 0, unroll=4)
+
+
+def forward_kernel(
+    recv_ref, high_ref, low_ref, weight_ref, out_ref, modes_ref, cells_ref, mixed_ref
+):
+    to_plane_modes(recv_ref, high_ref, low_ref, cells_ref, modes_ref)
+
+    for index in range(8):
+        half = index // 4
+        mode = index % 4
+        lanes = pl.ds(half * 128, 128)
+        real = jnp.zeros((CP, 128), f32)
+        imag = jnp.zeros((CP, 128), f32)
+        for ci in range(C):
+            sr = modes_ref[ci, pl.ds(mode, 1), lanes]
+            si = modes_ref[ci, pl.ds(mode + 4, 1), lanes]
+            wr = weight_ref[0, half, ci * 4 + mode]
+            wi = weight_ref[1, half, ci * 4 + mode]
+            real = real + (wr * sr - wi * si)
+            imag = imag + (wr * si + wi * sr)
+        mixed_ref[half, pl.ds(mode, C, stride=8), :] = real[:C]
+        mixed_ref[half, pl.ds(mode + 4, C, stride=8), :] = imag[:C]
+    mixed = jnp.concatenate([mixed_ref[0], mixed_ref[1]], axis=1)
+    to_plane_cells(mixed, high_ref, low_ref, cells_ref, out_ref)
+
+
+def backward_kernel(
+    recv_ref, high_ref, low_ref, weight_ref, sums_ref, out_ref, modes_ref, cells_ref, flat_ref, mixed_ref
+):
+    to_plane_modes(recv_ref, high_ref, low_ref, cells_ref, modes_ref)
+    for half in range(2):
+        flat_ref[half, pl.ds(0, C * 8), :] = modes_ref[:, :, pl.ds(half * 128, 128)].reshape(C * 8, 128)
+        flat_ref[half, pl.ds(C * 8, (CP - C) * 8), :] = jnp.zeros(((CP - C) * 8, 128), f32)
+
+    for index in range(8):
+        half = index // 4
+        mode = index % 4
+        lanes = pl.ds(half * 128, 128)
+        br = flat_ref[half, pl.ds(mode, CP, stride=8), :]
+        bi = flat_ref[half, pl.ds(mode + 4, CP, stride=8), :]
+        for ci in range(C):
+            wr = weight_ref[0, half, ci * 4 + mode]
+            wi = weight_ref[1, half, ci * 4 + mode]
+            real = jnp.sum(wr * br + wi * bi, axis=0, keepdims=True)
+            imag = jnp.sum(wr * bi - wi * br, axis=0, keepdims=True)
+            mixed_ref[pl.ds(ci * 8 + mode, 1), lanes] = real
+            mixed_ref[pl.ds(ci * 8 + mode + 4, 1), lanes] = imag
+    to_plane_cells(mixed_ref[...], high_ref, low_ref, cells_ref, out_ref)
+    tail = jnp.broadcast_to(sums_ref[...][None], (out_ref.shape[0], 8, 128))
+    for j in range(4):
+        out_ref[:, j, :, pl.ds(C * 32, 128)] = tail
+
+
+def gradient_kernel(forward_ref, backward_ref, out_ref, flat_ref, wide_ref):
+    part = pl.program_id(0)
+    flat_ref[...] = backward_ref[...].reshape(C * 8, 128)
+
+    for mode in range(4):
+        br = flat_ref[pl.ds(mode, C, stride=8), :]
+        bi = flat_ref[pl.ds(mode + 4, C, stride=8), :]
+        first = jnp.where(part == 0, br, bi)
+        second = jnp.where(part == 0, bi, -br)
+        for ci in range(C):
+            sr = forward_ref[ci, pl.ds(mode, 1), :]
+            si = forward_ref[ci, pl.ds(mode + 4, 1), :]
+            value = first * sr + second * si
+            value = jnp.concatenate([value, jnp.zeros((128 - C, 128), f32)])
+            wide_ref[pl.ds(ci * 4 + mode, 128, stride=PAIRS), :] = value.T
+    out_ref[0, 0] = wide_ref[:, pl.ds(0, C)]
+
+
+def activation(hidden):
+    cumulative = 0.5 * (1.0 + lax.erf(hidden * half_root))
+    slopes = cumulative + hidden * density_norm * jnp.exp(-0.5 * hidden * hidden)
+    return (hidden * cumulative, slopes)
+
+
+def layer_kernel(
+    recv_ref, table_ref, cells_ref, mix_ref, bias_ref, cotangent_ref,
+    out_ref, gradient_ref, sent_ref, high_ref, low_ref, total_ref,
+):
+    step = pl.program_id(0)
+
+    @pl.when(step == 0)
+    def _():
+        high, low = split(recv_ref[...].T)
+        high_ref[...] = high
+        low_ref[...] = low
+
+    table = table_ref[...]
+    hidden = (
+        dot(high_ref[...], table, NN)
+        + dot(low_ref[...], table, NN)
+        + dot(mix_ref[...], cells_ref[...], NN)
+        + bias_ref[...]
+    )
+    activated, slopes = activation(hidden)
+    out_ref[...] = activated.astype(bf16)
+    gradient = (cotangent_ref[...].astype(f32) * slopes).astype(bf16)
+    gradient_ref[...] = gradient
+    partial = dot(table, gradient, NT_DIMS)
+
+    @pl.when(step == 0)
+    def _():
+        total_ref[...] = partial
+
+    @pl.when(step > 0)
+    def _():
+        total_ref[...] += partial
+
+    @pl.when(step == pl.num_programs(0) - 1)
+    def _():
+        sent_ref[...] = total_ref[...].reshape(sent_ref.shape)
+
+
+def sums_kernel(cells_ref, gradient_ref, out_ref):
+    rows = C * 32
+    gram = dot(cells_ref[...], gradient_ref[...], NT_DIMS)
+    row = lax.broadcasted_iota(jnp.int32, (rows, rows), 0)
+    column = lax.broadcasted_iota(jnp.int32, (rows, rows), 1)
+    kept = jnp.where(row % 32 == column % 32, gram, 0.0)
+    folded = jnp.sum(kept.reshape(C, 32, rows), axis=1)
+    ones = jnp.ones((8, ZT), bf16)
+    bias = dot(ones, gradient_ref[...], NT_DIMS)
+    values = jnp.concatenate([folded, bias[:4]], axis=0)
+    owner = lax.broadcasted_iota(jnp.int32, (rows, 32), 0) // 32
+    slot = lax.broadcasted_iota(jnp.int32, (rows, 32), 1)
+    chooser = (owner == slot).astype(f32)
+    small = lax.dot_general(
+        values, chooser, (NN, ((), ())), precision=highest, preferred_element_type=f32
+    )
+    out_ref[...] = jnp.concatenate(
+        [small[0:8], small[8:16], small[16:24], jnp.zeros((8, 32), f32)], axis=1
+    )
+
+
+def final_kernel(recv_ref, table_ref, gradient_ref, mix_ref, out_ref, sums_ref, high_ref, low_ref):
+    step = pl.program_id(0)
+
+    @pl.when(step == 0)
+    def _():
+        devices = recv_ref.shape[0]
+        values = recv_ref[:, :, pl.ds(0, C * 32)].reshape(devices * 8, C * 32)
+        high, low = split(values.T)
+        high_ref[...] = high
+        low_ref[...] = low
+        sums_ref[...] = jnp.sum(recv_ref[:, :, pl.ds(C * 32, 128)], axis=0)
+
+    table = table_ref[...]
+    out_ref[...] = (
+        dot(high_ref[...], table, NN)
+        + dot(low_ref[...], table, NN)
+        + dot(mix_ref[...], gradient_ref[...], NN)
+    ).astype(bf16)
+
+
+def spread(weight):
+    owner = np.arange(C * 32) // 32
+    chooser = jnp.asarray((owner[:, None] == np.arange(C)[None, :]).astype(np.float32), bf16)
+    wide = dot(dot(chooser, weight, NN).astype(bf16), chooser, NT_DIMS)
+    place = jnp.arange(C * 32) % 32
+    return jnp.where(place[:, None] == place[None, :], wide, 0.0).astype(bf16)
+
+
+def exchange(values):
+    return lax.all_to_all(values, ("gx", "gy"), split_axis=0, concat_axis=0, tiled=True)
+
+
+def cost(flops, nbytes):
+    return pl.CostEstimate(flops=int(flops), bytes_accessed=int(nbytes), transcendentals=0)
+
+
+def fast_on_device(features, spectral_weight, pointwise_weight, pointwise_bias, cotangent):
+    first_local = features.shape[1]
+    second_local = features.shape[2]
+    first_groups = lax.axis_size("gx")
+    second_groups = lax.axis_size("gy")
+    devices = first_groups * second_groups
+    local = first_local * second_local
+    rows = C * local
+    cells = devices * local
+    quads = devices // 4
+    depth = jnp.asarray(depth_rows(devices)).astype(bf16)
+    plane = plane_table(first_groups, second_groups, first_local, second_local)
+    plane_high_np = plane.astype(jnp.bfloat16)
+    plane_low_np = (plane - plane_high_np.astype(np.float64)).astype(jnp.bfloat16)
+    plane_high = jnp.asarray(plane_high_np)
+    plane_low = jnp.asarray(plane_low_np)
+    flat = features.reshape(rows, ZT)
+    sent_shape = jax.ShapeDtypeStruct((devices, 8, rows), f32)
+    quad_shape = jax.ShapeDtypeStruct((quads, 4, 8, rows), f32)
+    modes_shape = jax.ShapeDtypeStruct((C, 8, AB), f32)
+
+    sent = pl.pallas_call(
+        depth_kernel,
+        out_shape=sent_shape,
+        in_specs=[whole(), whole()],
+        out_specs=whole(),
+        compiler_params=compiler(),
+        name="depth",
+    )(depth, flat)
+    received = exchange(sent)
+
+    stored = spectral_weight.transpose(0, 1, 2, 3, 5, 4).reshape(2, 2, 128 * PAIRS, C)
+    weight = pl.pallas_call(
+        weight_kernel,
+        out_shape=jax.ShapeDtypeStruct((2, 2, PAIRS, CP, 128), f32),
+        grid=(2, 2),
+        in_specs=[pl.BlockSpec((1, 1, 128 * PAIRS, C), lambda k, h: (k, h, 0, 0))],
+        out_specs=pl.BlockSpec((1, 1, PAIRS, CP, 128), lambda k, h: (k, h, 0, 0, 0)),
+        scratch_shapes=[pltpu.VMEM((128 * PAIRS, 128), f32)],
+        compiler_params=compiler(),
+        cost_estimate=cost(1e6, 25e6),
+        name="weights",
+    )(stored)
+    mix_back = spread(pointwise_weight)
+    mix_ahead = spread(pointwise_weight.T)
+    bias = jnp.broadcast_to(pointwise_bias[:, None], (C, local)).reshape(rows, 1)
+
+    back_out, modes = pl.pallas_call(
+        forward_kernel,
+        out_shape=(quad_shape, modes_shape),
+        in_specs=[whole()] * 4,
+        out_specs=(whole(), whole()),
+        scratch_shapes=[pltpu.VMEM((C * 8, cells), f32), pltpu.VMEM((2, C * 8, 128), f32)],
+        compiler_params=compiler(),
+        name="forward_modes",
+    )(received.reshape(quads, 4, 8, rows), plane_high, plane_low, weight)
+    returned = exchange(back_out.reshape(devices, 8, rows)).reshape(2 * MZT, rows)
+
+    blocks = ZT // BLOCK
+    column = pl.BlockSpec((rows, BLOCK), lambda s: (0, s))
+    table_column = pl.BlockSpec((2 * MZT, BLOCK), lambda s: (0, s))
+    layer_output, hidden_gradient, sent_back = pl.pallas_call(
+        layer_kernel,
+        out_shape=(
+            jax.ShapeDtypeStruct((rows, ZT), bf16),
+            jax.ShapeDtypeStruct((rows, ZT), bf16),
+            sent_shape,
+        ),
+        grid=(blocks,),
+        in_specs=[
+            pl.BlockSpec((2 * MZT, rows), lambda s: (0, 0)),
+            table_column,
+            column,
+            pl.BlockSpec((rows, rows), lambda s: (0, 0)),
+            pl.BlockSpec((rows, 1), lambda s: (0, 0)),
+            column,
+        ],
+        out_specs=(column, column, pl.BlockSpec((devices, 8, rows), lambda s: (0, 0, 0))),
+        scratch_shapes=[
+            pltpu.VMEM((rows, 2 * MZT), bf16),
+            pltpu.VMEM((rows, 2 * MZT), bf16),
+            pltpu.VMEM((2 * MZT, rows), f32),
+        ],
+        compiler_params=compiler(),
+        name="layer",
+    )(returned, depth, flat, mix_ahead, bias, cotangent.reshape(rows, ZT))
+    received_back = exchange(sent_back)
+
+    sums = pl.pallas_call(
+        sums_kernel,
+        out_shape=jax.ShapeDtypeStruct((8, 128), f32),
+        in_specs=[whole()] * 2,
+        out_specs=whole(),
+        compiler_params=compiler(),
+        cost_estimate=cost(1e9, 3e6),
+        name="sums",
+    )(flat, hidden_gradient)
+
+    wide = rows + 128
+    back_cells, back_modes = pl.pallas_call(
+        backward_kernel,
+        out_shape=(jax.ShapeDtypeStruct((quads, 4, 8, wide), f32), modes_shape),
+        in_specs=[whole()] * 5,
+        out_specs=(whole(), whole()),
+        scratch_shapes=[
+            pltpu.VMEM((C * 8, cells), f32),
+            pltpu.VMEM((2, CP * 8, 128), f32),
+            pltpu.VMEM((C * 8, AB), f32),
+        ],
+        compiler_params=compiler(),
+        name="backward_modes",
+    )(received_back.reshape(quads, 4, 8, rows), plane_high, plane_low, weight, sums)
+    returned_back = exchange(back_cells.reshape(devices, 8, wide))
+
+    gradient = pl.pallas_call(
+        gradient_kernel,
+        out_shape=jax.ShapeDtypeStruct((2, 2, 128 * PAIRS, C), f32),
+        grid=(2, 2),
+        in_specs=[
+            pl.BlockSpec((C, 8, 128), lambda k, h: (0, 0, h)),
+            pl.BlockSpec((C, 8, 128), lambda k, h: (0, 0, h)),
+        ],
+        out_specs=pl.BlockSpec((1, 1, 128 * PAIRS, C), lambda k, h: (k, h, 0, 0)),
+        scratch_shapes=[pltpu.VMEM((C * 8, 128), f32), pltpu.VMEM((128 * PAIRS, 128), f32)],
+        compiler_params=compiler(),
+        cost_estimate=cost(1e6, 25e6),
+        name="spectral_gradient",
+    )(modes, back_modes)
+    spectral_gradient = gradient.reshape(2, MX, MY, C, 4, C).transpose(0, 1, 2, 3, 5, 4)
+
+    features_gradient, totals = pl.pallas_call(
+        final_kernel,
+        out_shape=(jax.ShapeDtypeStruct((rows, ZT), bf16), jax.ShapeDtypeStruct((8, 128), f32)),
+        grid=(blocks,),
+        in_specs=[
+            pl.BlockSpec((devices, 8, wide), lambda s: (0, 0, 0)),
+            table_column,
+            column,
+            pl.BlockSpec((rows, rows), lambda s: (0, 0)),
+        ],
+        out_specs=(column, pl.BlockSpec((8, 128), lambda s: (0, 0))),
+        scratch_shapes=[
+            pltpu.VMEM((rows, 2 * MZT), bf16),
+            pltpu.VMEM((rows, 2 * MZT), bf16),
+        ],
+        compiler_params=compiler(),
+        name="features_gradient",
+    )(returned_back, depth, hidden_gradient, mix_back)
+
+    scaling = 1.0 / math.sqrt(cells * ZT)
+    pointwise_gradient = (
+        jnp.concatenate([totals[:, 0:C], totals[:, 32 : 32 + C], totals[:4, 64 : 64 + C]]) * scaling
+    )
+    bias_gradient = totals[4, 64 : 64 + C] * scaling
+    return (
+        layer_output.reshape(features.shape),
+        features_gradient.reshape(features.shape),
+        spectral_gradient,
+        pointwise_gradient,
+        bias_gradient,
+    )
 
 
 def kept_frequencies(length, mode_count):
@@ -48,7 +545,7 @@
     return entries.reshape(NZ * NT, 2, MZ * MT).astype(jnp.bfloat16)
 
 
-def activation(hidden):
+def wide_activation(hidden):
     cumulative = 0.5 * (1.0 + lax.erf(hidden * half_root))
     slopes = cumulative + hidden * density_norm * jnp.exp(-0.5 * hidden * hidden)
     return (hidden * cumulative, slopes)
@@ -125,7 +622,7 @@
         "ab,axys->bxys", pointwise_weight, features, preferred_element_type=jnp.float32
     )
     hidden = spectral + pointwise + pointwise_bias[:, None, None, None]
-    activated, slopes = activation(hidden)
+    activated, slopes = wide_activation(hidden)
     layer_output = activated.astype(jnp.bfloat16)
     hidden_gradient = (cotangent.astype(jnp.float32) * slopes).astype(jnp.bfloat16)
     weight_terms = jnp.einsum(
@@ -155,9 +652,19 @@
     )
 
 
+def place(features, spectral_weight, pointwise_weight, pointwise_bias, cotangent):
+    fits = (
+        spectral_weight.shape[5] == 4
+        and features.shape[1] * features.shape[2] == 32
+        and features.shape[3] == ZT
+    )
+    run = fast_on_device if fits else on_device
+    return run(features, spectral_weight, pointwise_weight, pointwise_bias, cotangent)
+
+
 def solution(mesh):
     return jax.shard_map(
-        on_device,
+        place,
         mesh=mesh,
         in_specs=(
             P(None, "gx", "gy", None),

time: 492 us -> 131 us (0.27); the launches traced: 485 us -> 130 us
  matrix products: 192 us -> 2.81 us
  local copies, waits for them, and re-layouts: 167 us -> 6.15 us
  Pallas kernels: 0 us -> 61.8 us
  other arithmetic: 47.1 us -> 1.88 us
  blocking collectives: 40.8 us -> 0 us
  waiting for transfers between devices: 14.5 us -> 38.7 us
    dot_general x23 -> x2, matrix products: 192 us -> 2.81 us  [dot(): lax.dot_general(left, right, (dims, ((), ())), preferred_element_type=f32)]
    pallas_call x0 -> x8, Pallas kernels: none -> 61.8 us  [the longest x1 15 us: fast_on_device(): pl.pallas_call(weight_kernel, out_shape=jax.ShapeDtypeStruct((2, 2, PAIRS...]
    squeeze x9 -> x0, local copies, waits for them, and re-layouts: 61.3 us -> none  [the longest x2 33.4 us: mix_forward(): weights[0]]
    unnamed x75 -> x14, local copies, waits for them, and re-layouts: 44.3 us -> 3.42 us
    psum x1 -> x0, blocking collectives: 40.8 us -> none  [on_device(): lax.psum((weight_terms, bias_terms), ('gx', 'gy'))]
    another operation x7 -> x0, other arithmetic: 28.6 us -> none  [the longest x2 25.2 us: weight_gradient(): return jnp.stack([real_out, imaginary])]
    all_to_all x7 -> x0, local copies, waits for them, and re-layouts: 26.5 us -> none  [the longest x5 16.6 us: to_modes(): lax.all_to_all(flattened, ('gx', 'gy'), split_axis=3, concat_axis=2, tile...]
    all_to_all x4, waiting for transfers between devices: 14.5 us -> 38.7 us  [exchange(): lax.all_to_all(values, ('gx', 'gy'), split_axis=0, concat_axis=0, tiled=T...]
  transfers between devices with their start and end apart: 4 -> 4, of which waited for: 1 -> 4; matrix products, arithmetic and copies ran while one was open for 20% -> 3% of each run, Pallas kernels for 0% -> 24%
where the time goes in v1:
time: 131 us; the launch traced here: 130 us
  Pallas kernels  61.8 us (47%)
  waiting for transfers between devices  38.7 us (30%)
  starting transfers between devices  17.8 us (14%)
  local copies, waits for them, and re-layouts  6.15 us (5%)
  matrix products  2.81 us (2%)
  other arithmetic  1.88 us (1%)
    all_to_all x4, waiting for transfers between devices, exchange(): lax.all_to_all(values, ('gx', 'gy'), split_axis=0, concat_axis=0, tiled=T...  38.7 us
    all_to_all x4, starting transfers between devices, exchange(): lax.all_to_all(values, ('gx', 'gy'), split_axis=0, concat_axis=0, tiled=T...  17.8 us
    pallas_call x1, Pallas kernels, fast_on_device(): pl.pallas_call(weight_kernel, out_shape=jax.ShapeDtypeStruct((2, 2, PAIRS...  15 us
    pallas_call x1, Pallas kernels, fast_on_device(): pl.pallas_call(gradient_kernel, out_shape=jax.ShapeDtypeStruct((2, 2, 128...  12.4 us
    pallas_call x1, Pallas kernels, fast_on_device(): pl.pallas_call(layer_kernel, out_shape=(jax.ShapeDtypeStruct((rows, ZT),...  8.06 us
    pallas_call x1, Pallas kernels, fast_on_device(): pl.pallas_call(backward_kernel, out_shape=(jax.ShapeDtypeStruct((quads, 4...  6.93 us
    pallas_call x1, Pallas kernels, fast_on_device(): pl.pallas_call(forward_kernel, out_shape=(quad_shape, modes_shape), in_sp...  6.68 us
    pallas_call x1, Pallas kernels, fast_on_device(): pl.pallas_call(final_kernel, out_shape=(jax.ShapeDtypeStruct((rows, ZT),...  5.56 us
  transfers between devices with their start and end apart: 4, of which 4 were waited for; matrix products, arithmetic and copies ran while one was open for 3% of the time, Pallas kernels for 24%

profile of v1, /device:TPU:0, one launch (start us, length us, event | category | flops | bytes accessed | tf_op | source)
XLA Modules:
  0.0 129.9 jit_solution(8476072131828161067)
XLA Ops:
  0.6 0.0 copy-start
  0.6 2.9 %depth.1 = f32[32,8,640]{2,1,0:T(8,128)} custom-call(bf16[256,1024]{1,0:T(8,128)(2,1)} %constant.42.table_ref, bf16[640,1024]{1,0:T(8,128)(2,1)} %bitcast.25), custom_call_target="tpu_custom_call" | custom-call | tf_op jit(solution)/shard_map/depth/pallas_call | solution.py:378
  3.6 7.3 %all-to-all-start = ((f32[32,8,640]{2,1,0:T(8,128)}), f32[32,8,640]{2,1,0:T(8,128)S(1)}, u32[]{:S(2)}, u32[]{:S(2)}) async-start(f32[32,8,640]{2,1,0:T(8,128)} %depth.1), calls=%async_computation | async-start | bytes 1310720 | tf_op jit(solution)/shard_map/all_to_all | solution.py:350
  10.9 15.0 %weights.1.weight_ref = f32[2,2,80,24,128]{4,3,2,1,0:T(8,128)} custom-call(f32[2,2,10240,20]{3,2,1,0:T(8,128)} %bitcast.23), custom_call_target="tpu_custom_call" | custom-call | flops 1000000 | bytes 25000000 | tf_op jit(solution)/shard_map/weights/pallas_call | solution.py:389
  25.9 3.0 %all-to-all-done = f32[32,8,640]{2,1,0:T(8,128)S(1)} async-done(((f32[32,8,640]{2,1,0:T(8,128)}), f32[32,8,640]{2,1,0:T(8,128)S(1)}, u32[]{:S(2)}, u32[]{:S(2)}) %all-to-all-start) | async-done | bytes 655392 | tf_op jit(solution)/shard_map/all_to_all | solution.py:350
  28.9 0.8 copy-done.3
  29.7 6.7 %forward_modes.1 = (f32[8,4,8,640]{3,2,1,0:T(8,128)}, f32[20,8,256]{2,1,0:T(8,128)}) custom-call(f32[8,4,8,640]{3,2,1,0:T(8,128)} %bitcast.29, bf16[512,1024]{1,0:T(8,128)(2,1)} %constant.36.clone.high_ref, bf16[512,1024]{1,0:T(8,128)(2,1)} %constant.37.clone.low_ref, f32[2,2,80,24,128]{4,3,2,1,0:T(8,128)} %weights.1.weight_ref), custom_call_target="tpu_custom_call" | custom-call | tf_op jit(solution)/shard_map/forward_modes/pallas_call | solution.py:404
  36.4 3.4 %all-to-all-start.1 = ((f32[32,8,640]{2,1,0:T(8,128)}), f32[32,8,640]{2,1,0:T(8,128)S(1)}, u32[]{:S(2)}, u32[]{:S(2)}) async-start(f32[32,8,640]{2,1,0:T(8,128)} %bitcast.33), calls=%async_computation.1 | async-start | bytes 1310720 | tf_op jit(solution)/shard_map/all_to_all | solution.py:350
  39.8 0.0 copy-done.5
  39.9 0.1 broadcast_in_dim.8
  39.9 1.1 reshape.79.bias_ref
  41.0 0.0 copy-done
  41.0 0.0 copy-done.6
  41.0 1.4 %fusion.mix_ref = bf16[640,640]{1,0:T(8,128)(2,1)} fusion(bf16[640,20]{1,0:T(8,128)(2,1)S(1)} %copy-done.6, bf16[20,20]{1,0:T(8,128)(2,1)S(1)} %copy-done, s32[640]{0:T(1024)S(1)} %add_select_fusion), kind=kOutput, calls=%fused_computation.2 | convolution fusion | flops 18137600 | bytes 848160 | tf_op jit(solution)/shard_map/dot_general | solution.py:81
  42.4 15.4 %all-to-all-done.1 = f32[32,8,640]{2,1,0:T(8,128)S(1)} async-done(((f32[32,8,640]{2,1,0:T(8,128)}), f32[32,8,640]{2,1,0:T(8,128)S(1)}, u32[]{:S(2)}, u32[]{:S(2)}) %all-to-all-start.1) | async-done | bytes 655392 | tf_op jit(solution)/shard_map/all_to_all | solution.py:350
  57.8 0.8 copy-done.2
  58.7 8.1 %layer.1 = (bf16[640,1024]{1,0:T(8,128)(2,1)}, bf16[640,1024]{1,0:T(8,128)(2,1)}, f32[32,8,640]{2,1,0:T(8,128)}) custom-call(f32[256,640]{1,0:T(8,128)} %bitcast.28, bf16[256,1024]{1,0:T(8,128)(2,1)} %constant.42.table_ref, bf16[640,1024]{1,0:T(8,128)(2,1)} %bitcast.26, bf16[640,640]{1,0:T(8,128)(2,1)} %fusion.mix_ref, f32[640,1]{1,0:T(8,128)} %reshape.79.bias_ref, ...), custom_call_target="tpu_custom_call" | custom-call | tf_op jit(solution)/shard_map/layer/pallas_call | solution.py:418
  66.7 3.4 %all-to-all-start.2 = ((f32[32,8,640]{2,1,0:T(8,128)}), f32[32,8,640]{2,1,0:T(8,128)S(1)}, u32[]{:S(2)}, u32[]{:S(2)}) async-start(f32[32,8,640]{2,1,0:T(8,128)} %get-tuple-element.16), calls=%async_computation.2 | async-start | bytes 1310720 | tf_op jit(solution)/shard_map/all_to_all | solution.py:350
  70.2 4.3 %sums.1.sums_ref = f32[8,128]{1,0:T(8,128)} custom-call(bf16[640,1024]{1,0:T(8,128)(2,1)} %bitcast.27, bf16[640,1024]{1,0:T(8,128)(2,1)} %get-tuple-element.17.gradient_ref), custom_call_target="tpu_custom_call" | custom-call | flops 1000000000 | bytes 3000000 | tf_op jit(solution)/shard_map/sums/pallas_call | solution.py:445
  74.5 13.7 %all-to-all-done.2 = f32[32,8,640]{2,1,0:T(8,128)S(1)} async-done(((f32[32,8,640]{2,1,0:T(8,128)}), f32[32,8,640]{2,1,0:T(8,128)S(1)}, u32[]{:S(2)}, u32[]{:S(2)}) %all-to-all-start.2) | async-done | bytes 655392 | tf_op jit(solution)/shard_map/all_to_all | solution.py:350
  88.2 0.8 copy-done.4
  89.0 6.9 %backward_modes.1 = (f32[8,4,8,768]{3,2,1,0:T(8,128)}, f32[20,8,256]{2,1,0:T(8,128)}) custom-call(f32[8,4,8,640]{3,2,1,0:T(8,128)} %bitcast.30, bf16[512,1024]{1,0:T(8,128)(2,1)} %constant.36.clone.high_ref, bf16[512,1024]{1,0:T(8,128)(2,1)} %constant.37.clone.low_ref, f32[2,2,80,24,128]{4,3,2,1,0:T(8,128)} %weights.1.weight_ref, f32[8,128]{1,0:T(8,128)} %sums.1.sums_ref), custom_call_target="tpu_custom_call" | custom-call | tf_op jit(solution)/shard_map/backward_modes/pallas_call | solution.py:456
  95.9 3.6 %all-to-all-start.3 = ((f32[32,8,768]{2,1,0:T(8,128)}), f32[32,8,768]{2,1,0:T(8,128)S(1)}, u32[]{:S(2)}, u32[]{:S(2)}) async-start(f32[32,8,768]{2,1,0:T(8,128)} %bitcast.32), calls=%async_computation.3 | async-start | bytes 1572864 | tf_op jit(solution)/shard_map/all_to_all | solution.py:350
  99.5 1.4 %fusion.1.mix_ref = bf16[640,640]{1,0:T(8,128)(2,1)} fusion(bf16[640,20]{1,0:T(8,128)(2,1)S(1)} %copy-done.6, bf16[20,20]{1,0:T(8,128)(2,1)S(1)} %copy-done, s32[640]{0:T(1024)S(1)} %add_select_fusion), kind=kOutput, calls=%fused_computation.3 | convolution fusion | flops 18137600 | bytes 848160 | tf_op jit(solution)/shard_map/dot_general | solution.py:81
  100.9 12.4 %spectral_gradient.1 = f32[2,2,10240,20]{3,2,1,0:T(8,128)} custom-call(f32[20,8,256]{2,1,0:T(8,128)} %get-tuple-element.20.forward_ref, f32[20,8,256]{2,1,0:T(8,128)} %get-tuple-element.21.backward_ref), custom_call_target="tpu_custom_call" | custom-call | flops 1000000 | bytes 25000000 | tf_op jit(solution)/shard_map/spectral_gradient/pallas_call | solution.py:471
  113.3 6.6 %all-to-all-done.3.recv_ref = f32[32,8,768]{2,1,0:T(8,128)S(1)} async-done(((f32[32,8,768]{2,1,0:T(8,128)}), f32[32,8,768]{2,1,0:T(8,128)S(1)}, u32[]{:S(2)}, u32[]{:S(2)}) %all-to-all-start.3) | async-done | bytes 786464 | tf_op jit(solution)/shard_map/all_to_all | solution.py:350
  119.9 0.9 copy-done.1
  120.8 5.6 %features_gradient.1 = (bf16[640,1024]{1,0:T(8,128)(2,1)}, f32[8,128]{1,0:T(8,128)}) custom-call(f32[32,8,768]{2,1,0:T(8,128)} %copy-done.1, bf16[256,1024]{1,0:T(8,128)(2,1)} %constant.42.table_ref, bf16[640,1024]{1,0:T(8,128)(2,1)} %get-tuple-element.17.gradient_ref, bf16[640,640]{1,0:T(8,128)(2,1)} %fusion.1.mix_ref), custom_call_target="tpu_custom_call" | custom-call | tf_op jit(solution)/shard_map/features_gradient/pallas_call | solution.py:487
  126.4 0.8 slice.14
  127.1 0.8 fusion.5
  128.0 1.3 multiply_bitcast_fusion
  129.2 0.6 maximum_multiply_fusion
  (7 shorter events, 0.0 us)
Async XLA Ops:
  0.6 40.4 %copy-start = (bf16[20,20]{1,0:T(8,128)(2,1)S(1)}, bf16[20,20]{1,0:T(8,128)(2,1)}, u32[]{:S(2)}) copy-start(bf16[20,20]{1,0:T(8,128)(2,1)} %param.12) | copy-start | bytes 2404
  3.6 25.3 %all-to-all-start = ((f32[32,8,640]{2,1,0:T(8,128)}), f32[32,8,640]{2,1,0:T(8,128)S(1)}, u32[]{:S(2)}, u32[]{:S(2)}) async-start(f32[32,8,640]{2,1,0:T(8,128)} %depth.1), calls=%async_computation | async-start | bytes 1310720 | tf_op jit(solution)/shard_map/all_to_all | solution.py:350
  28.9 0.8 copy-start.3
  29.7 10.1 %copy-start.5 = (f32[20]{0:T(128)S(1)}, f32[20]{0:T(128)}, u32[]{:S(2)}) copy-start(f32[20]{0:T(128)} %param.13) | copy-start | bytes 244
  36.4 4.6 %copy-start.6 = (bf16[640,20]{1,0:T(8,128)(2,1)S(1)}, bf16[640,20]{1,0:T(8,128)(2,1)}, u32[]{:S(2)}) copy-start(bf16[640,20]{1,0:T(8,128)(2,1)} %constant.38.clone) | copy-start | bytes 76804
  36.4 21.4 %all-to-all-start.1 = ((f32[32,8,640]{2,1,0:T(8,128)}), f32[32,8,640]{2,1,0:T(8,128)S(1)}, u32[]{:S(2)}, u32[]{:S(2)}) async-start(f32[32,8,640]{2,1,0:T(8,128)} %bitcast.33), calls=%async_computation.1 | async-start | bytes 1310720 | tf_op jit(solution)/shard_map/all_to_all | solution.py:350
  57.8 0.8 copy-start.2
  66.7 21.4 %all-to-all-start.2 = ((f32[32,8,640]{2,1,0:T(8,128)}), f32[32,8,640]{2,1,0:T(8,128)S(1)}, u32[]{:S(2)}, u32[]{:S(2)}) async-start(f32[32,8,640]{2,1,0:T(8,128)} %get-tuple-element.16), calls=%async_computation.2 | async-start | bytes 1310720 | tf_op jit(solution)/shard_map/all_to_all | solution.py:350
  88.2 0.8 copy-start.4
  95.9 24.0 %all-to-all-start.3 = ((f32[32,8,768]{2,1,0:T(8,128)}), f32[32,8,768]{2,1,0:T(8,128)S(1)}, u32[]{:S(2)}, u32[]{:S(2)}) async-start(f32[32,8,768]{2,1,0:T(8,128)} %bitcast.32), calls=%async_computation.3 | async-start | bytes 1572864 | tf_op jit(solution)/shard_map/all_to_all | solution.py:350
  119.9 0.9 copy-start.1

commit v2 on v1

--- a/solution.py
+++ b/solution.py
@@ -52,26 +52,6 @@
     return rows.reshape(2 * MZT, ZT).astype(np.float32)
 
 
-def plane_table(first_groups, second_groups, first_local, second_local):
-    nx = first_groups * first_local
-    ny = second_groups * second_local
-    kx = frequencies(nx, MX)
-    ky = frequencies(ny, MY)
-    gx, gy, cx, cy = np.meshgrid(
-        np.arange(first_groups),
-        np.arange(second_groups),
-        np.arange(first_local),
-        np.arange(second_local),
-        indexing="ij",
-    )
-    x = (gx * first_local + cx).reshape(-1)
-    y = (gy * second_local + cy).reshape(-1)
-    ax = 2.0 * np.pi / nx * (kx[:, None] * x[None, :] % nx)
-    ay = 2.0 * np.pi / ny * (ky[:, None] * y[None, :] % ny)
-    angle = (ax[:, None, :] + ay[None, :, :]).reshape(AB, nx * ny)
-    return np.concatenate([np.cos(angle), np.sin(angle)]) / math.sqrt(nx * ny)
-
-
 def split(values):
     high = values.astype(bf16)
     return high, (values - high.astype(f32)).astype(bf16)
@@ -86,17 +66,47 @@
 TN = ((0,), (0,))
 
 
-def compiler(limit=None):
-    return pltpu.CompilerParams(vmem_limit_bytes=limit or 60 * 1024 * 1024)
+def start(source, target, sem):
+    copy = pltpu.make_async_copy(source, target, sem)
+    copy.start()
+    return copy
+
+
+def compiler(mebibytes):
+    return pltpu.CompilerParams(vmem_limit_bytes=mebibytes * 1024 * 1024)
 
 
 def whole(memory=pltpu.VMEM):
     return pl.BlockSpec(memory_space=memory)
 
 
-def depth_kernel(table_ref, cells_ref, out_ref):
-    out = dot(table_ref[...], cells_ref[...], NT_DIMS)
-    out_ref[...] = out.reshape(out_ref.shape)
+def in_hbm(shape, dtype):
+    return pltpu.HBM(shape, dtype)
+
+
+def from_hbm(values):
+    return pltpu.with_memory_space_constraint(values, pltpu.HBM)
+
+
+def depth_kernel(table_hbm, cells_hbm, out_hbm, table_ref, cells_ref, out_ref, sems):
+    table_copy = start(table_hbm, table_ref, sems.at[0])
+    groups = cells_ref.shape[0] // 128
+    blocks = [pl.ds(g * 128, 128) for g in range(groups)]
+    arriving = [
+        start(cells_hbm.at[block], cells_ref.at[block], sems.at[1 + g])
+        for g, block in enumerate(blocks)
+    ]
+    table_copy.wait()
+    leaving = []
+    for g, block in enumerate(blocks):
+        arriving[g].wait()
+        out = dot(table_ref[...], cells_ref[block, :], NT_DIMS)
+        out_ref[:, :, block] = out.reshape(out_ref.shape[0], 8, 128)
+        leaving.append(
+            start(out_ref.at[:, :, block], out_hbm.at[:, :, block], sems.at[1 + groups + g])
+        )
+    for copy in leaving:
+        copy.wait()
 
 
 def swap_blocks(tiles):
@@ -142,7 +152,7 @@
     modes_ref[...] = cosine + row_sign(sine.shape, 1.0) * pltpu.roll(sine, 4, 1)
 
 
-def to_plane_cells(mixed, high_ref, low_ref, cells_ref, out_ref):
+def to_plane_cells(mixed, high_ref, low_ref, cells_ref, out_ref, out_hbm, sems):
     high, low = split(mixed)
 
     def product(rows):
@@ -158,6 +168,7 @@
         cosine + row_sign(sine.shape, -1.0) * pltpu.roll(sine, 4, 1)
     ).reshape(cells_ref.shape)
     groups = out_ref.shape[0]
+    copies = []
     for group in range(C // 4):
         tiles = [
             jnp.stack(
@@ -168,8 +179,13 @@
             )
             for i in range(4)
         ]
+        lanes = pl.ds(group * 128, 128)
         for j, tile in enumerate(swap_blocks(tiles)):
-            out_ref[:, j, :, pl.ds(group * 128, 128)] = tile
+            out_ref[:, j, :, lanes] = tile
+        copies.append(
+            start(out_ref.at[:, :, :, lanes], out_hbm.at[:, :, :, lanes], sems.at[group])
+        )
+    return copies
 
 
 def weight_kernel(weight_ref, out_ref, wide_ref):
@@ -178,40 +194,63 @@
 
     def step(pair, carry):
         rows = wide_ref[pl.ds(pair, 128, stride=PAIRS), :]
-        out_ref[0, 0, pair] = jnp.where(row < C, rows.T[:CP], 0.0)
+        out_ref[0, pair % 4, 0, pair // 4] = jnp.where(row < C, rows.T[:CP], 0.0)
         return carry
 
     lax.fori_loop(0, PAIRS, step, 0, unroll=4)
 
 
+def fetch_weights(weight_hbm, weight_ref, sems):
+    return [
+        start(
+            weight_hbm.at[index // 4, index % 4], weight_ref.at[index // 4, index % 4], sems.at[13 + index]
+        )
+        for index in range(8)
+    ]
+
+
 def forward_kernel(
-    recv_ref, high_ref, low_ref, weight_ref, out_ref, modes_ref, cells_ref, mixed_ref
+    recv_ref, high_ref, low_ref, weight_hbm, out_hbm, modes_out,
+    weight_ref, modes_ref, cells_ref, mixed_ref, out_ref, sems,
 ):
+    weights = fetch_weights(weight_hbm, weight_ref, sems)
     to_plane_modes(recv_ref, high_ref, low_ref, cells_ref, modes_ref)
+    copies = [start(modes_ref, modes_out, sems.at[11])]
 
     for index in range(8):
         half = index // 4
         mode = index % 4
         lanes = pl.ds(half * 128, 128)
+        weights[index].wait()
         real = jnp.zeros((CP, 128), f32)
         imag = jnp.zeros((CP, 128), f32)
         for ci in range(C):
             sr = modes_ref[ci, pl.ds(mode, 1), lanes]
             si = modes_ref[ci, pl.ds(mode + 4, 1), lanes]
-            wr = weight_ref[0, half, ci * 4 + mode]
-            wi = weight_ref[1, half, ci * 4 + mode]
+            wr = weight_ref[half, mode, 0, ci]
+            wi = weight_ref[half, mode, 1, ci]
             real = real + (wr * sr - wi * si)
             imag = imag + (wr * si + wi * sr)
         mixed_ref[half, pl.ds(mode, C, stride=8), :] = real[:C]
         mixed_ref[half, pl.ds(mode + 4, C, stride=8), :] = imag[:C]
     mixed = jnp.concatenate([mixed_ref[0], mixed_ref[1]], axis=1)
-    to_plane_cells(mixed, high_ref, low_ref, cells_ref, out_ref)
+    copies += to_plane_cells(mixed, high_ref, low_ref, cells_ref, out_ref, out_hbm, sems)
+    for copy in copies:
+        copy.wait()
 
 
 def backward_kernel(
-    recv_ref, high_ref, low_ref, weight_ref, sums_ref, out_ref, modes_ref, cells_ref, flat_ref, mixed_ref
+    recv_ref, high_ref, low_ref, weight_hbm, sums_ref, out_hbm, modes_out,
+    weight_ref, modes_ref, cells_ref, flat_ref, mixed_ref, out_ref, sems,
 ):
+    weights = fetch_weights(weight_hbm, weight_ref, sems)
+    tail = jnp.broadcast_to(sums_ref[...][None], (out_ref.shape[0], 8, 128))
+    lanes = pl.ds(C * 32, 128)
+    for j in range(4):
+        out_ref[:, j, :, lanes] = tail
+    copies = [start(out_ref.at[:, :, :, lanes], out_hbm.at[:, :, :, lanes], sems.at[12])]
     to_plane_modes(recv_ref, high_ref, low_ref, cells_ref, modes_ref)
+    copies.append(start(modes_ref, modes_out, sems.at[11]))
     for half in range(2):
         flat_ref[half, pl.ds(0, C * 8), :] = modes_ref[:, :, pl.ds(half * 128, 128)].reshape(C * 8, 128)
         flat_ref[half, pl.ds(C * 8, (CP - C) * 8), :] = jnp.zeros(((CP - C) * 8, 128), f32)
@@ -220,19 +259,19 @@
         half = index // 4
         mode = index % 4
         lanes = pl.ds(half * 128, 128)
+        weights[index].wait()
         br = flat_ref[half, pl.ds(mode, CP, stride=8), :]
         bi = flat_ref[half, pl.ds(mode + 4, CP, stride=8), :]
         for ci in range(C):
-            wr = weight_ref[0, half, ci * 4 + mode]
-            wi = weight_ref[1, half, ci * 4 + mode]
+            wr = weight_ref[half, mode, 0, ci]
+            wi = weight_ref[half, mode, 1, ci]
             real = jnp.sum(wr * br + wi * bi, axis=0, keepdims=True)
             imag = jnp.sum(wr * bi - wi * br, axis=0, keepdims=True)
             mixed_ref[pl.ds(ci * 8 + mode, 1), lanes] = real
             mixed_ref[pl.ds(ci * 8 + mode + 4, 1), lanes] = imag
-    to_plane_cells(mixed_ref[...], high_ref, low_ref, cells_ref, out_ref)
-    tail = jnp.broadcast_to(sums_ref[...][None], (out_ref.shape[0], 8, 128))
-    for j in range(4):
-        out_ref[:, j, :, pl.ds(C * 32, 128)] = tail
+    copies += to_plane_cells(mixed_ref[...], high_ref, low_ref, cells_ref, out_ref, out_hbm, sems)
+    for copy in copies:
+        copy.wait()
 
 
 def gradient_kernel(forward_ref, backward_ref, out_ref, flat_ref, wide_ref):
@@ -259,42 +298,57 @@
     return (hidden * cumulative, slopes)
 
 
+def pointwise_kernel(dims, weight_ref, bias_ref, cells_ref, out_ref):
+    rows = C * 32
+    owner = lax.broadcasted_iota(jnp.int32, (rows, C), 0) // 32
+    slot = lax.broadcasted_iota(jnp.int32, (rows, C), 1)
+    chooser = (owner == slot).astype(f32).astype(bf16)
+    row = lax.broadcasted_iota(jnp.int32, (rows, rows), 0)
+    column = lax.broadcasted_iota(jnp.int32, (rows, rows), 1)
+    tall = dot(chooser, weight_ref[...], dims).astype(bf16)
+    wide = dot(tall, chooser, NT_DIMS)
+    mix = jnp.where(row % 32 == column % 32, wide, 0.0).astype(bf16)
+    kept = jnp.where(owner == slot, jnp.broadcast_to(bias_ref[...], (rows, C)), 0.0)
+    bias = jnp.sum(kept, axis=1, keepdims=True)
+    for s in range(ZT // BLOCK):
+        lanes = pl.ds(s * BLOCK, BLOCK)
+        out_ref[:, lanes] = dot(mix, cells_ref[:, lanes], NN) + bias
+
+
 def layer_kernel(
-    recv_ref, table_ref, cells_ref, mix_ref, bias_ref, cotangent_ref,
-    out_ref, gradient_ref, sent_ref, high_ref, low_ref, total_ref,
+    recv_ref, table_ref, local_hbm, cotangent_hbm,
+    out_hbm, gradient_hbm, sent_hbm,
+    local_ref, cotangent_ref, out_ref, gradient_ref, sent_ref, sems,
 ):
-    step = pl.program_id(0)
-
-    @pl.when(step == 0)
-    def _():
-        high, low = split(recv_ref[...].T)
-        high_ref[...] = high
-        low_ref[...] = low
-
-    table = table_ref[...]
-    hidden = (
-        dot(high_ref[...], table, NN)
-        + dot(low_ref[...], table, NN)
-        + dot(mix_ref[...], cells_ref[...], NN)
-        + bias_ref[...]
-    )
-    activated, slopes = activation(hidden)
-    out_ref[...] = activated.astype(bf16)
-    gradient = (cotangent_ref[...].astype(f32) * slopes).astype(bf16)
-    gradient_ref[...] = gradient
-    partial = dot(table, gradient, NT_DIMS)
-
-    @pl.when(step == 0)
-    def _():
-        total_ref[...] = partial
-
-    @pl.when(step > 0)
-    def _():
-        total_ref[...] += partial
-
-    @pl.when(step == pl.num_programs(0) - 1)
-    def _():
-        sent_ref[...] = total_ref[...].reshape(sent_ref.shape)
+    blocks = ZT // BLOCK
+    columns = [pl.ds(s * BLOCK, BLOCK) for s in range(blocks)]
+    local_copies = []
+    cotangent_copies = []
+    for s, lanes in enumerate(columns):
+        local_copies.append(start(local_hbm.at[:, lanes], local_ref.at[:, lanes], sems.at[2 + s]))
+        cotangent_copies.append(
+            start(cotangent_hbm.at[:, lanes], cotangent_ref.at[:, lanes], sems.at[6 + s])
+        )
+    high, low = split(recv_ref[...].T)
+    total = None
+    copies = []
+    for s, lanes in enumerate(columns):
+        table = table_ref[:, lanes]
+        spectral = dot(high, table, NN) + dot(low, table, NN)
+        local_copies[s].wait()
+        activated, slopes = activation(spectral + local_ref[:, lanes])
+        out_ref[:, lanes] = activated.astype(bf16)
+        copies.append(start(out_ref.at[:, lanes], out_hbm.at[:, lanes], sems.at[10 + s]))
+        cotangent_copies[s].wait()
+        gradient = (cotangent_ref[:, lanes].astype(f32) * slopes).astype(bf16)
+        gradient_ref[:, lanes] = gradient
+        copies.append(start(gradient_ref.at[:, lanes], gradient_hbm.at[:, lanes], sems.at[14 + s]))
+        partial = dot(table, gradient, NT_DIMS)
+        total = partial if total is None else total + partial
+    sent_ref[...] = total.reshape(sent_ref.shape)
+    copies.append(start(sent_ref, sent_hbm, sems.at[18]))
+    for copy in copies:
+        copy.wait()
 
 
 def sums_kernel(cells_ref, gradient_ref, out_ref):
@@ -318,32 +372,65 @@
     )
 
 
-def final_kernel(recv_ref, table_ref, gradient_ref, mix_ref, out_ref, sums_ref, high_ref, low_ref):
-    step = pl.program_id(0)
-
-    @pl.when(step == 0)
-    def _():
-        devices = recv_ref.shape[0]
-        values = recv_ref[:, :, pl.ds(0, C * 32)].reshape(devices * 8, C * 32)
-        high, low = split(values.T)
-        high_ref[...] = high
-        low_ref[...] = low
-        sums_ref[...] = jnp.sum(recv_ref[:, :, pl.ds(C * 32, 128)], axis=0)
-
-    table = table_ref[...]
-    out_ref[...] = (
-        dot(high_ref[...], table, NN)
-        + dot(low_ref[...], table, NN)
-        + dot(mix_ref[...], gradient_ref[...], NN)
-    ).astype(bf16)
-
-
-def spread(weight):
-    owner = np.arange(C * 32) // 32
-    chooser = jnp.asarray((owner[:, None] == np.arange(C)[None, :]).astype(np.float32), bf16)
-    wide = dot(dot(chooser, weight, NN).astype(bf16), chooser, NT_DIMS)
-    place = jnp.arange(C * 32) % 32
-    return jnp.where(place[:, None] == place[None, :], wide, 0.0).astype(bf16)
+def final_kernel(
+    scaling, recv_ref, table_ref, local_hbm, out_hbm, weight_ref, bias_ref,
+    local_ref, out_ref, sems,
+):
+    blocks = ZT // BLOCK
+    columns = [pl.ds(s * BLOCK, BLOCK) for s in range(blocks)]
+    local_copies = [
+        start(local_hbm.at[:, lanes], local_ref.at[:, lanes], sems.at[2 + s])
+        for s, lanes in enumerate(columns)
+    ]
+    devices = recv_ref.shape[0]
+    values = recv_ref[:, :, pl.ds(0, C * 32)].reshape(devices * 8, C * 32)
+    high, low = split(values.T)
+    copies = []
+    for s, lanes in enumerate(columns):
+        table = table_ref[:, lanes]
+        spectral = dot(high, table, NN) + dot(low, table, NN)
+        local_copies[s].wait()
+        out_ref[:, lanes] = (spectral + local_ref[:, lanes]).astype(bf16)
+        copies.append(start(out_ref.at[:, lanes], out_hbm.at[:, lanes], sems.at[6 + s]))
+    sums = jnp.sum(recv_ref[:, :, pl.ds(C * 32, 128)], axis=0) * scaling
+    weight_ref[pl.ds(0, 8), :] = sums[:, 0:C]
+    weight_ref[pl.ds(8, 8), :] = sums[:, 32 : 32 + C]
+    weight_ref[pl.ds(16, 4), :] = sums[:4, 64 : 64 + C]
+    bias_ref[...] = sums[4:5, 64 : 64 + C]
+    for copy in copies:
+        copy.wait()
+
+
+def plane_kernel(first_local, second_local, first_groups, second_groups, high_out, low_out, part_ref):
+    nx = first_local * first_groups
+    ny = second_local * second_groups
+    cells = nx * ny
+    local = first_local * second_local
+    cell = lax.broadcasted_iota(jnp.int32, (16, cells), 1)
+    mode = lax.broadcasted_iota(jnp.int32, (16, cells), 0)
+    group = cell // local
+    x = (group // second_groups) * first_local + (cell % local) // second_local
+    y = (group % second_groups) * second_local + cell % second_local
+
+    def waves(length, count, position):
+        frequency = jnp.where(mode < count // 2, mode, mode + length - count)
+        phase = (frequency * position) % length
+        phase = jnp.where(phase >= length // 2, phase - length, phase)
+        angle = phase.astype(f32) * (2.0 * math.pi / length)
+        return jnp.cos(angle) / math.sqrt(length), jnp.sin(angle) / math.sqrt(length)
+
+    for slot, values in enumerate((*waves(nx, MX, x), *waves(ny, MY, y))):
+        part_ref[slot] = values
+    cy = part_ref[2]
+    sy = part_ref[3]
+    for kx in range(MX):
+        cx = part_ref[0, pl.ds(kx, 1), :]
+        sx = part_ref[1, pl.ds(kx, 1), :]
+        for offset, values in ((0, cx * cy - sx * sy), (AB, sx * cy + cx * sy)):
+            high, low = split(values)
+            place = pl.ds(offset + kx * MY, MY)
+            high_out[place, :] = high
+            low_out[place, :] = low
 
 
 def exchange(values):
@@ -364,113 +451,137 @@
     rows = C * local
     cells = devices * local
     quads = devices // 4
-    depth = jnp.asarray(depth_rows(devices)).astype(bf16)
-    plane = plane_table(first_groups, second_groups, first_local, second_local)
-    plane_high_np = plane.astype(jnp.bfloat16)
-    plane_low_np = (plane - plane_high_np.astype(np.float64)).astype(jnp.bfloat16)
-    plane_high = jnp.asarray(plane_high_np)
-    plane_low = jnp.asarray(plane_low_np)
-    flat = features.reshape(rows, ZT)
-    sent_shape = jax.ShapeDtypeStruct((devices, 8, rows), f32)
-    quad_shape = jax.ShapeDtypeStruct((quads, 4, 8, rows), f32)
-    modes_shape = jax.ShapeDtypeStruct((C, 8, AB), f32)
+    depth = jnp.asarray(depth_rows(devices).astype(jnp.bfloat16))
+    flat = from_hbm(features.reshape(rows, ZT))
+    hbm = whole(pltpu.HBM)
+    near = whole()
 
     sent = pl.pallas_call(
         depth_kernel,
-        out_shape=sent_shape,
-        in_specs=[whole(), whole()],
-        out_specs=whole(),
-        compiler_params=compiler(),
+        out_shape=in_hbm((devices, 8, rows), f32),
+        in_specs=[hbm, hbm],
+        out_specs=hbm,
+        scratch_shapes=[
+            pltpu.VMEM((2 * MZT, ZT), bf16),
+            pltpu.VMEM((rows, ZT), bf16),
+            pltpu.VMEM((devices, 8, rows), f32),
+            pltpu.SemaphoreType.DMA((1 + 2 * (rows // 128),)),
+        ],
+        compiler_params=compiler(8),
         name="depth",
-    )(depth, flat)
+    )(from_hbm(depth), flat)
     received = exchange(sent)
 
     stored = spectral_weight.transpose(0, 1, 2, 3, 5, 4).reshape(2, 2, 128 * PAIRS, C)
     weight = pl.pallas_call(
         weight_kernel,
-        out_shape=jax.ShapeDtypeStruct((2, 2, PAIRS, CP, 128), f32),
+        out_shape=in_hbm((2, 4, 2, C, CP, 128), f32),
         grid=(2, 2),
         in_specs=[pl.BlockSpec((1, 1, 128 * PAIRS, C), lambda k, h: (k, h, 0, 0))],
-        out_specs=pl.BlockSpec((1, 1, PAIRS, CP, 128), lambda k, h: (k, h, 0, 0, 0)),
+        out_specs=pl.BlockSpec((1, 4, 1, C, CP, 128), lambda k, h: (h, 0, k, 0, 0, 0)),
         scratch_shapes=[pltpu.VMEM((128 * PAIRS, 128), f32)],
-        compiler_params=compiler(),
+        compiler_params=compiler(22),
         cost_estimate=cost(1e6, 25e6),
         name="weights",
-    )(stored)
-    mix_back = spread(pointwise_weight)
-    mix_ahead = spread(pointwise_weight.T)
-    bias = jnp.broadcast_to(pointwise_bias[:, None], (C, local)).reshape(rows, 1)
-
+    )(from_hbm(stored))
+    high, low = pl.pallas_call(
+        functools.partial(plane_kernel, first_local, second_local, first_groups, second_groups),
+        out_shape=(jax.ShapeDtypeStruct((2 * AB, cells), bf16),) * 2,
+        in_specs=[],
+        out_specs=[near] * 2,
+        scratch_shapes=[pltpu.VMEM((4, 16, cells), f32)],
+        compiler_params=compiler(6),
+        cost_estimate=cost(1e8, 2e6),
+        name="planes",
+    )()
+
+    def pointwise(dims, bias, values, name):
+        return pl.pallas_call(
+            functools.partial(pointwise_kernel, dims),
+            out_shape=in_hbm((rows, ZT), f32),
+            in_specs=[near] * 3,
+            out_specs=near,
+            compiler_params=compiler(12),
+            cost_estimate=cost(1e9, 5e6),
+            name=name,
+        )(pointwise_weight, bias, values)
+
+    plane_scratch = [
+        pltpu.VMEM((2, 4, 2, C, CP, 128), f32),
+        pltpu.VMEM((C, 8, AB), f32),
+        pltpu.VMEM((C * 8, cells), f32),
+    ]
     back_out, modes = pl.pallas_call(
         forward_kernel,
-        out_shape=(quad_shape, modes_shape),
-        in_specs=[whole()] * 4,
-        out_specs=(whole(), whole()),
-        scratch_shapes=[pltpu.VMEM((C * 8, cells), f32), pltpu.VMEM((2, C * 8, 128), f32)],
-        compiler_params=compiler(),
+        out_shape=(in_hbm((quads, 4, 8, rows), f32), in_hbm((C, 8, AB), f32)),
+        in_specs=[near, near, near, hbm],
+        out_specs=(hbm, hbm),
+        scratch_shapes=plane_scratch
+        + [
+            pltpu.VMEM((2, C * 8, 128), f32),
+            pltpu.VMEM((quads, 4, 8, rows), f32),
+            pltpu.SemaphoreType.DMA((21,)),
+        ],
+        compiler_params=compiler(20),
         name="forward_modes",
-    )(received.reshape(quads, 4, 8, rows), plane_high, plane_low, weight)
+    )(received.reshape(quads, 4, 8, rows), high, low, from_hbm(weight))
     returned = exchange(back_out.reshape(devices, 8, rows)).reshape(2 * MZT, rows)
 
-    blocks = ZT // BLOCK
-    column = pl.BlockSpec((rows, BLOCK), lambda s: (0, s))
-    table_column = pl.BlockSpec((2 * MZT, BLOCK), lambda s: (0, s))
+    local_ahead = pointwise(NT_DIMS, pointwise_bias.reshape(1, C), flat, "pointwise_ahead")
     layer_output, hidden_gradient, sent_back = pl.pallas_call(
         layer_kernel,
         out_shape=(
-            jax.ShapeDtypeStruct((rows, ZT), bf16),
-            jax.ShapeDtypeStruct((rows, ZT), bf16),
-            sent_shape,
+            in_hbm((rows, ZT), bf16),
+            in_hbm((rows, ZT), bf16),
+            in_hbm((devices, 8, rows), f32),
         ),
-        grid=(blocks,),
-        in_specs=[
-            pl.BlockSpec((2 * MZT, rows), lambda s: (0, 0)),
-            table_column,
-            column,
-            pl.BlockSpec((rows, rows), lambda s: (0, 0)),
-            pl.BlockSpec((rows, 1), lambda s: (0, 0)),
-            column,
+        in_specs=[near, near, hbm, hbm],
+        out_specs=(hbm, hbm, hbm),
+        scratch_shapes=[
+            pltpu.VMEM((rows, ZT), f32),
+            pltpu.VMEM((rows, ZT), bf16),
+            pltpu.VMEM((rows, ZT), bf16),
+            pltpu.VMEM((rows, ZT), bf16),
+            pltpu.VMEM((devices, 8, rows), f32),
+            pltpu.SemaphoreType.DMA((19,)),
         ],
-        out_specs=(column, column, pl.BlockSpec((devices, 8, rows), lambda s: (0, 0, 0))),
-        scratch_shapes=[
-            pltpu.VMEM((rows, 2 * MZT), bf16),
-            pltpu.VMEM((rows, 2 * MZT), bf16),
-            pltpu.VMEM((2 * MZT, rows), f32),
-        ],
-        compiler_params=compiler(),
+        compiler_params=compiler(24),
         name="layer",
-    )(returned, depth, flat, mix_ahead, bias, cotangent.reshape(rows, ZT))
+    )(returned, depth, from_hbm(local_ahead), from_hbm(cotangent.reshape(rows, ZT)))
     received_back = exchange(sent_back)
 
     sums = pl.pallas_call(
         sums_kernel,
         out_shape=jax.ShapeDtypeStruct((8, 128), f32),
-        in_specs=[whole()] * 2,
-        out_specs=whole(),
-        compiler_params=compiler(),
+        in_specs=[near] * 2,
+        out_specs=near,
+        compiler_params=compiler(12),
         cost_estimate=cost(1e9, 3e6),
         name="sums",
-    )(flat, hidden_gradient)
-
+    )(flat, from_hbm(hidden_gradient))
+
+    local_back = pointwise(NN, jnp.zeros((1, C), f32), from_hbm(hidden_gradient), "pointwise_back")
     wide = rows + 128
     back_cells, back_modes = pl.pallas_call(
         backward_kernel,
-        out_shape=(jax.ShapeDtypeStruct((quads, 4, 8, wide), f32), modes_shape),
-        in_specs=[whole()] * 5,
-        out_specs=(whole(), whole()),
-        scratch_shapes=[
-            pltpu.VMEM((C * 8, cells), f32),
+        out_shape=(in_hbm((quads, 4, 8, wide), f32), in_hbm((C, 8, AB), f32)),
+        in_specs=[near, near, near, hbm, near],
+        out_specs=(hbm, hbm),
+        scratch_shapes=plane_scratch
+        + [
             pltpu.VMEM((2, CP * 8, 128), f32),
             pltpu.VMEM((C * 8, AB), f32),
+            pltpu.VMEM((quads, 4, 8, wide), f32),
+            pltpu.SemaphoreType.DMA((21,)),
         ],
-        compiler_params=compiler(),
+        compiler_params=compiler(20),
         name="backward_modes",
-    )(received_back.reshape(quads, 4, 8, rows), plane_high, plane_low, weight, sums)
+    )(received_back.reshape(quads, 4, 8, rows), high, low, from_hbm(weight), sums)
     returned_back = exchange(back_cells.reshape(devices, 8, wide))
 
     gradient = pl.pallas_call(
         gradient_kernel,
-        out_shape=jax.ShapeDtypeStruct((2, 2, 128 * PAIRS, C), f32),
+        out_shape=in_hbm((2, 2, 128 * PAIRS, C), f32),
         grid=(2, 2),
         in_specs=[
             pl.BlockSpec((C, 8, 128), lambda k, h: (0, 0, h)),
@@ -478,42 +589,36 @@
         ],
         out_specs=pl.BlockSpec((1, 1, 128 * PAIRS, C), lambda k, h: (k, h, 0, 0)),
         scratch_shapes=[pltpu.VMEM((C * 8, 128), f32), pltpu.VMEM((128 * PAIRS, 128), f32)],
-        compiler_params=compiler(),
+        compiler_params=compiler(20),
         cost_estimate=cost(1e6, 25e6),
         name="spectral_gradient",
     )(modes, back_modes)
     spectral_gradient = gradient.reshape(2, MX, MY, C, 4, C).transpose(0, 1, 2, 3, 5, 4)
 
-    features_gradient, totals = pl.pallas_call(
-        final_kernel,
-        out_shape=(jax.ShapeDtypeStruct((rows, ZT), bf16), jax.ShapeDtypeStruct((8, 128), f32)),
-        grid=(blocks,),
-        in_specs=[
-            pl.BlockSpec((devices, 8, wide), lambda s: (0, 0, 0)),
-            table_column,
-            column,
-            pl.BlockSpec((rows, rows), lambda s: (0, 0)),
+    features_gradient, pointwise_gradient, bias_gradient = pl.pallas_call(
+        functools.partial(final_kernel, 1.0 / math.sqrt(cells * ZT)),
+        out_shape=(
+            in_hbm((rows, ZT), bf16),
+            jax.ShapeDtypeStruct((C, C), f32),
+            jax.ShapeDtypeStruct((1, C), f32),
+        ),
+        in_specs=[near, near, hbm],
+        out_specs=(hbm, near, near),
+        scratch_shapes=[
+            pltpu.VMEM((rows, ZT), f32),
+            pltpu.VMEM((rows, ZT), bf16),
+            pltpu.SemaphoreType.DMA((10,)),
         ],
-        out_specs=(column, pl.BlockSpec((8, 128), lambda s: (0, 0))),
-        scratch_shapes=[
-            pltpu.VMEM((rows, 2 * MZT), bf16),
-            pltpu.VMEM((rows, 2 * MZT), bf16),
-        ],
-        compiler_params=compiler(),
+        compiler_params=compiler(16),
         name="features_gradient",
-    )(returned_back, depth, hidden_gradient, mix_back)
-
-    scaling = 1.0 / math.sqrt(cells * ZT)
-    pointwise_gradient = (
-        jnp.concatenate([totals[:, 0:C], totals[:, 32 : 32 + C], totals[:4, 64 : 64 + C]]) * scaling
-    )
-    bias_gradient = totals[4, 64 : 64 + C] * scaling
+    )(returned_back, depth, from_hbm(local_back))
+
     return (
         layer_output.reshape(features.shape),
         features_gradient.reshape(features.shape),
         spectral_gradient,
         pointwise_gradient,
-        bias_gradient,
+        bias_gradient.reshape(C),
     )
 
 

time: 131 us -> 117 us (0.89)
  local copies, waits for them, and re-layouts: 6.15 us -> 0.03 us
  waiting for transfers between devices: 38.7 us -> 34.3 us
  matrix products: 2.81 us -> 0 us
  other arithmetic: 1.88 us -> 0 us
    all_to_all x4, waiting for transfers between devices: 38.7 us -> 34.3 us  [exchange(): lax.all_to_all(values, ('gx', 'gy'), split_axis=0, concat_axis=0, tiled=T...]
    unnamed x14 -> x10, local copies, waits for them, and re-layouts: 3.42 us -> 0.02 us
    dot_general x2 -> x0, matrix products: 2.81 us -> none  [dot(): lax.dot_general(left, right, (dims, ((), ())), preferred_element_type=f32)]
    mul x2 -> x0, other arithmetic: 1.87 us -> none  [the longest x1 1.27 us: fast_on_device(): bias_gradient = totals[4, 64:64 + C] * scaling]
    pallas_call x7 -> x10, Pallas kernels: 57.5 us -> 59.2 us  [the longest x1 15 us: fast_on_device(): pl.pallas_call(weight_kernel, out_shape=in_hbm((2, 4, 2, C, CP, 128), f32...]
    slice x2 -> x0, local copies, waits for them, and re-layouts: 1.59 us -> none  [the longest x1 0.83 us: fast_on_device(): totals[:, 0:C]]
  transfers between devices with their start and end apart: 4 -> 4, of which waited for: 4 -> 4; matrix products, arithmetic and copies ran while one was open for 3% -> 0% of each run, Pallas kernels for 24% -> 34%
where the time goes in v2:
time: 117 us; the launch traced here: 116 us
  Pallas kernels  62.9 us (54%)
  waiting for transfers between devices  34.3 us (29%)
  starting transfers between devices  18.4 us (16%)
    all_to_all x4, waiting for transfers between devices, exchange(): lax.all_to_all(values, ('gx', 'gy'), split_axis=0, concat_axis=0, tiled=T...  34.3 us
    all_to_all x4, starting transfers between devices, exchange(): lax.all_to_all(values, ('gx', 'gy'), split_axis=0, concat_axis=0, tiled=T...  18.4 us
    pallas_call x1, Pallas kernels, fast_on_device(): pl.pallas_call(weight_kernel, out_shape=in_hbm((2, 4, 2, C, CP, 128), f32...  15 us
    pallas_call x1, Pallas kernels, fast_on_device(): pl.pallas_call(gradient_kernel, out_shape=in_hbm((2, 2, 128 * PAIRS, C),...  11.5 us
    pallas_call x2, Pallas kernels, pointwise(): pl.pallas_call(functools.partial(pointwise_kernel, dims), out_shape=in_hb...  8.69 us
    pallas_call x1, Pallas kernels, fast_on_device(): pl.pallas_call(layer_kernel, out_shape=(in_hbm((rows, ZT), bf16), in_hbm(...  5.71 us
    pallas_call x1, Pallas kernels, fast_on_device(): pl.pallas_call(backward_kernel, out_shape=(in_hbm((quads, 4, 8, wide), f3...  4.62 us
    pallas_call x1, Pallas kernels, fast_on_device(): pl.pallas_call(forward_kernel, out_shape=(in_hbm((quads, 4, 8, rows), f32...  4.54 us
  transfers between devices with their start and end apart: 4, of which 4 were waited for; matrix products, arithmetic and copies ran while one was open for 0% of the time, Pallas kernels for 34%

profile of v2, /device:TPU:0, one launch (start us, length us, event | category | flops | bytes accessed | tf_op | source)
XLA Modules:
  0.0 116.5 jit_solution(7375857943272224278)
XLA Ops:
  0.6 3.8 %depth.1 = f32[32,8,640]{2,1,0:T(8,128)} custom-call(bf16[256,1024]{1,0:T(8,128)(2,1)} %constant.4.clone.table_hbm.table_ref, bf16[640,1024]{1,0:T(8,128)(2,1)} %bitcast.23), custom_call_target="tpu_custom_call" | custom-call | tf_op jit(solution)/shard_map/depth/pallas_call | solution.py:459
  4.5 7.3 %all-to-all-start = ((f32[32,8,640]{2,1,0:T(8,128)}), f32[32,8,640]{2,1,0:T(8,128)S(1)}, u32[]{:S(2)}, u32[]{:S(2)}) async-start(f32[32,8,640]{2,1,0:T(8,128)} %depth.1), calls=%async_computation | async-start | bytes 1310720 | tf_op jit(solution)/shard_map/all_to_all | solution.py:437
  11.8 15.0 %weights.1.weight_hbm = f32[2,4,2,20,24,128]{5,4,3,2,1,0:T(8,128)} custom-call(f32[2,2,10240,20]{3,2,1,0:T(8,128)} %bitcast.21), custom_call_target="tpu_custom_call" | custom-call | flops 1000000 | bytes 25000000 | tf_op jit(solution)/shard_map/weights/pallas_call | solution.py:476
  26.8 1.1 planes.1
  27.9 1.9 %all-to-all-done = f32[32,8,640]{2,1,0:T(8,128)S(1)} async-done(((f32[32,8,640]{2,1,0:T(8,128)}), f32[32,8,640]{2,1,0:T(8,128)S(1)}, u32[]{:S(2)}, u32[]{:S(2)}) %all-to-all-start) | async-done | bytes 655392 | tf_op jit(solution)/shard_map/all_to_all | solution.py:437
  29.8 0.0 copy-start.3
  29.8 0.0 copy-start.4
  29.8 4.5 %forward_modes.1 = (f32[8,4,8,640]{3,2,1,0:T(8,128)}, f32[20,8,256]{2,1,0:T(8,128)}) custom-call(f32[8,4,8,640]{3,2,1,0:T(8,128)S(1)} %bitcast.17, bf16[512,1024]{1,0:T(8,128)(2,1)S(1)} %get-tuple-element.17.high_ref, bf16[512,1024]{1,0:T(8,128)(2,1)S(1)} %get-tuple-element.18.low_ref, f32[2,4,2,20,24,128]{5,4,3,2,1,0:T(8,128)} %weights.1.weight_hbm), custom_call_target="tpu_custom_call" | custom-call | tf_op jit(solution)/shard_map/forward_modes/pallas_call | solution.py:514
  34.3 0.0 copy-start
  34.4 4.0 %all-to-all-start.1 = ((f32[32,8,640]{2,1,0:T(8,128)}), f32[32,8,640]{2,1,0:T(8,128)S(1)}, u32[]{:S(2)}, u32[]{:S(2)}) async-start(f32[32,8,640]{2,1,0:T(8,128)} %bitcast.28), calls=%async_computation.1 | async-start | bytes 1310720 | tf_op jit(solution)/shard_map/all_to_all | solution.py:437
  38.4 0.0 copy-done.3
  38.4 0.0 copy-done.4
  38.4 4.3 %pointwise_ahead.1.local_hbm = f32[640,1024]{1,0:T(8,128)} custom-call(bf16[20,20]{1,0:T(8,128)(2,1)S(1)} %copy-done.3, f32[1,20]{1,0:T(1,128)S(1)} %bitcast.20, bf16[640,1024]{1,0:T(8,128)(2,1)} %bitcast.24), custom_call_target="tpu_custom_call" | custom-call | flops 1000000000 | bytes 5000000 | tf_op jit(solution)/shard_map/pointwise_ahead/pallas_call | solution.py:499
  42.7 13.6 %all-to-all-done.1 = f32[32,8,640]{2,1,0:T(8,128)S(1)} async-done(((f32[32,8,640]{2,1,0:T(8,128)}), f32[32,8,640]{2,1,0:T(8,128)S(1)}, u32[]{:S(2)}, u32[]{:S(2)}) %all-to-all-start.1) | async-done | bytes 655392 | tf_op jit(solution)/shard_map/all_to_all | solution.py:437
  56.4 0.0 copy-done
  56.4 5.7 %layer.1 = (bf16[640,1024]{1,0:T(8,128)(2,1)}, bf16[640,1024]{1,0:T(8,128)(2,1)}, f32[32,8,640]{2,1,0:T(8,128)}) custom-call(f32[256,640]{1,0:T(8,128)S(1)} %bitcast.18, bf16[256,1024]{1,0:T(8,128)(2,1)S(1)} %copy-done, f32[640,1024]{1,0:T(8,128)} %pointwise_ahead.1.local_hbm, bf16[640,1024]{1,0:T(8,128)(2,1)} %bitcast.26), custom_call_target="tpu_custom_call" | custom-call | tf_op jit(solution)/shard_map/layer/pallas_call | solution.py:531
  62.1 3.6 %all-to-all-start.2 = ((f32[32,8,640]{2,1,0:T(8,128)}), f32[32,8,640]{2,1,0:T(8,128)S(1)}, u32[]{:S(2)}, u32[]{:S(2)}) async-start(f32[32,8,640]{2,1,0:T(8,128)} %get-tuple-element.21), calls=%async_computation.2 | async-start | bytes 1310720 | tf_op jit(solution)/shard_map/all_to_all | solution.py:437
  65.7 3.7 %sums.1.sums_ref = f32[8,128]{1,0:T(8,128)S(1)} custom-call(bf16[640,1024]{1,0:T(8,128)(2,1)} %bitcast.25, bf16[640,1024]{1,0:T(8,128)(2,1)} %get-tuple-element.22.gradient_ref.cells_ref), custom_call_target="tpu_custom_call" | custom-call | flops 1000000000 | bytes 3000000 | tf_op jit(solution)/shard_map/sums/pallas_call | solution.py:553
  69.4 14.1 %all-to-all-done.2 = f32[32,8,640]{2,1,0:T(8,128)S(1)} async-done(((f32[32,8,640]{2,1,0:T(8,128)}), f32[32,8,640]{2,1,0:T(8,128)S(1)}, u32[]{:S(2)}, u32[]{:S(2)}) %all-to-all-start.2) | async-done | bytes 655392 | tf_op jit(solution)/shard_map/all_to_all | solution.py:437
  83.5 4.6 %backward_modes.1 = (f32[8,4,8,768]{3,2,1,0:T(8,128)}, f32[20,8,256]{2,1,0:T(8,128)}) custom-call(f32[8,4,8,640]{3,2,1,0:T(8,128)S(1)} %bitcast.19, bf16[512,1024]{1,0:T(8,128)(2,1)S(1)} %get-tuple-element.17.high_ref, bf16[512,1024]{1,0:T(8,128)(2,1)S(1)} %get-tuple-element.18.low_ref, f32[2,4,2,20,24,128]{5,4,3,2,1,0:T(8,128)} %weights.1.weight_hbm, ...), custom_call_target="tpu_custom_call" | custom-call | tf_op jit(solution)/shard_map/backward_modes/pallas_call | solution.py:565
  88.1 0.0 copy-start.1
  88.1 0.0 copy-start.2
  88.1 3.4 %all-to-all-start.3 = ((f32[32,8,768]{2,1,0:T(8,128)}), f32[32,8,768]{2,1,0:T(8,128)S(1)}, u32[]{:S(2)}, u32[]{:S(2)}) async-start(f32[32,8,768]{2,1,0:T(8,128)} %bitcast.27), calls=%async_computation.3 | async-start | bytes 1572864 | tf_op jit(solution)/shard_map/all_to_all | solution.py:437
  91.6 4.3 %pointwise_back.1.local_hbm = f32[640,1024]{1,0:T(8,128)} custom-call(bf16[20,20]{1,0:T(8,128)(2,1)S(1)} %copy-done.3, f32[1,20]{1,0:T(1,128)S(1)} %broadcast_1_bias_ref.2.bias_ref, bf16[640,1024]{1,0:T(8,128)(2,1)} %get-tuple-element.22.gradient_ref.cells_ref), custom_call_target="tpu_custom_call" | custom-call | flops 1000000000 | bytes 5000000 | tf_op jit(solution)/shard_map/pointwise_back/pallas_call | solution.py:499
  95.9 0.0 copy-done.1
  95.9 0.0 copy-done.2
  95.9 11.5 %spectral_gradient.1 = f32[2,2,10240,20]{3,2,1,0:T(8,128)} custom-call(f32[20,8,256]{2,1,0:T(8,128)S(1)} %copy-done.1, f32[20,8,256]{2,1,0:T(8,128)S(1)} %copy-done.2), custom_call_target="tpu_custom_call" | custom-call | flops 1000000 | bytes 25000000 | tf_op jit(solution)/shard_map/spectral_gradient/pallas_call | solution.py:582
  107.4 4.7 %all-to-all-done.3.recv_ref = f32[32,8,768]{2,1,0:T(8,128)S(1)} async-done(((f32[32,8,768]{2,1,0:T(8,128)}), f32[32,8,768]{2,1,0:T(8,128)S(1)}, u32[]{:S(2)}, u32[]{:S(2)}) %all-to-all-start.3) | async-done | bytes 786464 | tf_op jit(solution)/shard_map/all_to_all | solution.py:437
  112.2 4.2 %features_gradient.1 = (bf16[640,1024]{1,0:T(8,128)(2,1)}, f32[20,20]{1,0:T(8,128)}, f32[1,20]{1,0:T(1,128)}) custom-call(f32[32,8,768]{2,1,0:T(8,128)S(1)} %all-to-all-done.3.recv_ref, bf16[256,1024]{1,0:T(8,128)(2,1)S(1)} %copy-done, f32[640,1024]{1,0:T(8,128)} %pointwise_back.1.local_hbm), custom_call_target="tpu_custom_call" | custom-call | tf_op jit(solution)/shard_map/features_gradient/pallas_call | solution.py:598
  (1 shorter events, 0.0 us)
Async XLA Ops:
  4.5 25.3 %all-to-all-start = ((f32[32,8,640]{2,1,0:T(8,128)}), f32[32,8,640]{2,1,0:T(8,128)S(1)}, u32[]{:S(2)}, u32[]{:S(2)}) async-start(f32[32,8,640]{2,1,0:T(8,128)} %depth.1), calls=%async_computation | async-start | bytes 1310720 | tf_op jit(solution)/shard_map/all_to_all | solution.py:437
  29.8 8.6 %copy-start.3 = (bf16[20,20]{1,0:T(8,128)(2,1)S(1)}, bf16[20,20]{1,0:T(8,128)(2,1)}, u32[]{:S(2)}) copy-start(bf16[20,20]{1,0:T(8,128)(2,1)} %weight_ref.3) | copy-start | bytes 2404
  29.8 8.6 %copy-start.4 = (f32[20]{0:T(128)S(1)}, f32[20]{0:T(128)}, u32[]{:S(2)}) copy-start(f32[20]{0:T(128)} %param.9) | copy-start | bytes 244
  34.3 22.0 %copy-start = (bf16[256,1024]{1,0:T(8,128)(2,1)S(1)}, bf16[256,1024]{1,0:T(8,128)(2,1)}, u32[]{:S(2)}) copy-start(bf16[256,1024]{1,0:T(8,128)(2,1)} %constant.4.clone.table_hbm.table_ref) | copy-start | bytes 1572868
  34.4 22.0 %all-to-all-start.1 = ((f32[32,8,640]{2,1,0:T(8,128)}), f32[32,8,640]{2,1,0:T(8,128)S(1)}, u32[]{:S(2)}, u32[]{:S(2)}) async-start(f32[32,8,640]{2,1,0:T(8,128)} %bitcast.28), calls=%async_computation.1 | async-start | bytes 1310720 | tf_op jit(solution)/shard_map/all_to_all | solution.py:437
  62.1 21.4 %all-to-all-start.2 = ((f32[32,8,640]{2,1,0:T(8,128)}), f32[32,8,640]{2,1,0:T(8,128)S(1)}, u32[]{:S(2)}, u32[]{:S(2)}) async-start(f32[32,8,640]{2,1,0:T(8,128)} %get-tuple-element.21), calls=%async_computation.2 | async-start | bytes 1310720 | tf_op jit(solution)/shard_map/all_to_all | solution.py:437
  88.1 7.8 %copy-start.1 = (f32[20,8,256]{2,1,0:T(8,128)S(1)}, f32[20,8,256]{2,1,0:T(8,128)}, u32[]{:S(2)}) copy-start(f32[20,8,256]{2,1,0:T(8,128)} %get-tuple-element.25.forward_ref) | copy-start | bytes 491524
  88.1 7.8 %copy-start.2 = (f32[20,8,256]{2,1,0:T(8,128)S(1)}, f32[20,8,256]{2,1,0:T(8,128)}, u32[]{:S(2)}) copy-start(f32[20,8,256]{2,1,0:T(8,128)} %get-tuple-element.26.backward_ref) | copy-start | bytes 491524
  88.1 24.0 %all-to-all-start.3 = ((f32[32,8,768]{2,1,0:T(8,128)}), f32[32,8,768]{2,1,0:T(8,128)S(1)}, u32[]{:S(2)}, u32[]{:S(2)}) async-start(f32[32,8,768]{2,1,0:T(8,128)} %bitcast.27), calls=%async_computation.3 | async-start | bytes 1572864 | tf_op jit(solution)/shard_map/all_to_all | solution.py:437

commit v3 on v2

--- a/solution.py
+++ b/solution.py
@@ -63,7 +63,6 @@
 
 NN = ((1,), (0,))
 NT_DIMS = ((1,), (1,))
-TN = ((0,), (0,))
 
 
 def start(source, target, sem):
@@ -197,7 +196,7 @@
         out_ref[0, pair % 4, 0, pair // 4] = jnp.where(row < C, rows.T[:CP], 0.0)
         return carry
 
-    lax.fori_loop(0, PAIRS, step, 0, unroll=4)
+    lax.fori_loop(0, PAIRS, step, 0, unroll=16)
 
 
 def fetch_weights(weight_hbm, weight_ref, sems):
@@ -240,17 +239,12 @@
 
 
 def backward_kernel(
-    recv_ref, high_ref, low_ref, weight_hbm, sums_ref, out_hbm, modes_out,
+    recv_ref, high_ref, low_ref, weight_hbm, out_hbm, modes_out,
     weight_ref, modes_ref, cells_ref, flat_ref, mixed_ref, out_ref, sems,
 ):
     weights = fetch_weights(weight_hbm, weight_ref, sems)
-    tail = jnp.broadcast_to(sums_ref[...][None], (out_ref.shape[0], 8, 128))
-    lanes = pl.ds(C * 32, 128)
-    for j in range(4):
-        out_ref[:, j, :, lanes] = tail
-    copies = [start(out_ref.at[:, :, :, lanes], out_hbm.at[:, :, :, lanes], sems.at[12])]
     to_plane_modes(recv_ref, high_ref, low_ref, cells_ref, modes_ref)
-    copies.append(start(modes_ref, modes_out, sems.at[11]))
+    copies = [start(modes_ref, modes_out, sems.at[11])]
     for half in range(2):
         flat_ref[half, pl.ds(0, C * 8), :] = modes_ref[:, :, pl.ds(half * 128, 128)].reshape(C * 8, 128)
         flat_ref[half, pl.ds(C * 8, (CP - C) * 8), :] = jnp.zeros(((CP - C) * 8, 128), f32)
@@ -298,16 +292,23 @@
     return (hidden * cumulative, slopes)
 
 
-def pointwise_kernel(dims, weight_ref, bias_ref, cells_ref, out_ref):
+def spread(weight, dims):
     rows = C * 32
     owner = lax.broadcasted_iota(jnp.int32, (rows, C), 0) // 32
     slot = lax.broadcasted_iota(jnp.int32, (rows, C), 1)
     chooser = (owner == slot).astype(f32).astype(bf16)
     row = lax.broadcasted_iota(jnp.int32, (rows, rows), 0)
     column = lax.broadcasted_iota(jnp.int32, (rows, rows), 1)
-    tall = dot(chooser, weight_ref[...], dims).astype(bf16)
+    tall = dot(chooser, weight, dims).astype(bf16)
     wide = dot(tall, chooser, NT_DIMS)
-    mix = jnp.where(row % 32 == column % 32, wide, 0.0).astype(bf16)
+    return jnp.where(row % 32 == column % 32, wide, 0.0).astype(bf16)
+
+
+def pointwise_kernel(weight_ref, bias_ref, cells_ref, out_ref):
+    rows = C * 32
+    owner = lax.broadcasted_iota(jnp.int32, (rows, C), 0) // 32
+    slot = lax.broadcasted_iota(jnp.int32, (rows, C), 1)
+    mix = spread(weight_ref[...], NT_DIMS)
     kept = jnp.where(owner == slot, jnp.broadcast_to(bias_ref[...], (rows, C)), 0.0)
     bias = jnp.sum(kept, axis=1, keepdims=True)
     for s in range(ZT // BLOCK):
@@ -351,8 +352,18 @@
         copy.wait()
 
 
-def sums_kernel(cells_ref, gradient_ref, out_ref):
+def products_kernel(weight_ref, cells_hbm, gradient_hbm, out_ref, local_hbm, cells_ref, gradient_ref, local_ref, sems):
+    gradient_copy = start(gradient_hbm, gradient_ref, sems.at[0])
+    cells_copy = start(cells_hbm, cells_ref, sems.at[1])
     rows = C * 32
+    mix = spread(weight_ref[...], NN)
+    gradient_copy.wait()
+    copies = []
+    for s in range(ZT // BLOCK):
+        lanes = pl.ds(s * BLOCK, BLOCK)
+        local_ref[:, lanes] = dot(mix, gradient_ref[:, lanes], NN)
+        copies.append(start(local_ref.at[:, lanes], local_hbm.at[:, lanes], sems.at[2 + s]))
+    cells_copy.wait()
     gram = dot(cells_ref[...], gradient_ref[...], NT_DIMS)
     row = lax.broadcasted_iota(jnp.int32, (rows, rows), 0)
     column = lax.broadcasted_iota(jnp.int32, (rows, rows), 1)
@@ -370,21 +381,30 @@
     out_ref[...] = jnp.concatenate(
         [small[0:8], small[8:16], small[16:24], jnp.zeros((8, 32), f32)], axis=1
     )
-
-
-def final_kernel(
-    scaling, recv_ref, table_ref, local_hbm, out_hbm, weight_ref, bias_ref,
-    local_ref, out_ref, sems,
-):
+    for copy in copies:
+        copy.wait()
+
+
+def total_kernel(scaling, own_ref, other_ref, weight_ref, bias_ref):
+    sums = (own_ref[...] + other_ref[...]) * scaling
+    weight_ref[pl.ds(0, 8), :] = sums[:, 0:C]
+    weight_ref[pl.ds(8, 8), :] = sums[:, 32 : 32 + C]
+    weight_ref[pl.ds(16, 4), :] = sums[:4, 64 : 64 + C]
+    bias_ref[...] = sums[4:5, 64 : 64 + C]
+
+
+def quad_kernel(own_ref, first_ref, second_ref, third_ref, out_ref):
+    out_ref[...] = (own_ref[...] + first_ref[...]) + (second_ref[...] + third_ref[...])
+
+
+def final_kernel(recv_ref, table_ref, local_hbm, out_hbm, local_ref, out_ref, sems):
     blocks = ZT // BLOCK
     columns = [pl.ds(s * BLOCK, BLOCK) for s in range(blocks)]
     local_copies = [
         start(local_hbm.at[:, lanes], local_ref.at[:, lanes], sems.at[2 + s])
         for s, lanes in enumerate(columns)
     ]
-    devices = recv_ref.shape[0]
-    values = recv_ref[:, :, pl.ds(0, C * 32)].reshape(devices * 8, C * 32)
-    high, low = split(values.T)
+    high, low = split(recv_ref[...].T)
     copies = []
     for s, lanes in enumerate(columns):
         table = table_ref[:, lanes]
@@ -392,11 +412,6 @@
         local_copies[s].wait()
         out_ref[:, lanes] = (spectral + local_ref[:, lanes]).astype(bf16)
         copies.append(start(out_ref.at[:, lanes], out_hbm.at[:, lanes], sems.at[6 + s]))
-    sums = jnp.sum(recv_ref[:, :, pl.ds(C * 32, 128)], axis=0) * scaling
-    weight_ref[pl.ds(0, 8), :] = sums[:, 0:C]
-    weight_ref[pl.ds(8, 8), :] = sums[:, 32 : 32 + C]
-    weight_ref[pl.ds(16, 4), :] = sums[:4, 64 : 64 + C]
-    bias_ref[...] = sums[4:5, 64 : 64 + C]
     for copy in copies:
         copy.wait()
 
@@ -435,6 +450,10 @@
 
 def exchange(values):
     return lax.all_to_all(values, ("gx", "gy"), split_axis=0, concat_axis=0, tiled=True)
+
+
+def partner(values, bit, devices):
+    return lax.ppermute(values, ("gx", "gy"), [(i, i ^ bit) for i in range(devices)])
 
 
 def cost(flops, nbytes):
@@ -495,17 +514,6 @@
         name="planes",
     )()
 
-    def pointwise(dims, bias, values, name):
-        return pl.pallas_call(
-            functools.partial(pointwise_kernel, dims),
-            out_shape=in_hbm((rows, ZT), f32),
-            in_specs=[near] * 3,
-            out_specs=near,
-            compiler_params=compiler(12),
-            cost_estimate=cost(1e9, 5e6),
-            name=name,
-        )(pointwise_weight, bias, values)
-
     plane_scratch = [
         pltpu.VMEM((2, 4, 2, C, CP, 128), f32),
         pltpu.VMEM((C, 8, AB), f32),
@@ -527,7 +535,15 @@
     )(received.reshape(quads, 4, 8, rows), high, low, from_hbm(weight))
     returned = exchange(back_out.reshape(devices, 8, rows)).reshape(2 * MZT, rows)
 
-    local_ahead = pointwise(NT_DIMS, pointwise_bias.reshape(1, C), flat, "pointwise_ahead")
+    local_ahead = pl.pallas_call(
+        pointwise_kernel,
+        out_shape=in_hbm((rows, ZT), f32),
+        in_specs=[near] * 3,
+        out_specs=near,
+        compiler_params=compiler(12),
+        cost_estimate=cost(1e9, 5e6),
+        name="pointwise_ahead",
+    )(pointwise_weight, pointwise_bias.reshape(1, C), flat)
     layer_output, hidden_gradient, sent_back = pl.pallas_call(
         layer_kernel,
         out_shape=(
@@ -550,34 +566,58 @@
     )(returned, depth, from_hbm(local_ahead), from_hbm(cotangent.reshape(rows, ZT)))
     received_back = exchange(sent_back)
 
-    sums = pl.pallas_call(
-        sums_kernel,
-        out_shape=jax.ShapeDtypeStruct((8, 128), f32),
+    sums, local_back = pl.pallas_call(
+        products_kernel,
+        out_shape=(jax.ShapeDtypeStruct((8, 128), f32), in_hbm((rows, ZT), f32)),
+        in_specs=[near, hbm, hbm],
+        out_specs=(near, hbm),
+        scratch_shapes=[
+            pltpu.VMEM((rows, ZT), bf16),
+            pltpu.VMEM((rows, ZT), bf16),
+            pltpu.VMEM((rows, ZT), f32),
+            pltpu.SemaphoreType.DMA((6,)),
+        ],
+        compiler_params=compiler(16),
+        cost_estimate=cost(2e9, 6e6),
+        name="products",
+    )(pointwise_weight, flat, from_hbm(hidden_gradient))
+
+    for bits in ((1, 2, 3), (4, 8, 12)):
+        parts = [partner(sums, bit, devices) for bit in bits]
+        sums = pl.pallas_call(
+            quad_kernel,
+            out_shape=jax.ShapeDtypeStruct((8, 128), f32),
+            in_specs=[near] * 4,
+            out_specs=near,
+            compiler_params=compiler(2),
+            name="quad_sum",
+        )(sums, *parts)
+    other = partner(sums, 16, devices)
+    pointwise_gradient, bias_gradient = pl.pallas_call(
+        functools.partial(total_kernel, 1.0 / math.sqrt(cells * ZT)),
+        out_shape=(jax.ShapeDtypeStruct((C, C), f32), jax.ShapeDtypeStruct((1, C), f32)),
         in_specs=[near] * 2,
-        out_specs=near,
-        compiler_params=compiler(12),
-        cost_estimate=cost(1e9, 3e6),
-        name="sums",
-    )(flat, from_hbm(hidden_gradient))
-
-    local_back = pointwise(NN, jnp.zeros((1, C), f32), from_hbm(hidden_gradient), "pointwise_back")
-    wide = rows + 128
+        out_specs=(near, near),
+        compiler_params=compiler(2),
+        name="total_sum",
+    )(sums, other)
+
     back_cells, back_modes = pl.pallas_call(
         backward_kernel,
-        out_shape=(in_hbm((quads, 4, 8, wide), f32), in_hbm((C, 8, AB), f32)),
-        in_specs=[near, near, near, hbm, near],
+        out_shape=(in_hbm((quads, 4, 8, rows), f32), in_hbm((C, 8, AB), f32)),
+        in_specs=[near, near, near, hbm],
         out_specs=(hbm, hbm),
         scratch_shapes=plane_scratch
         + [
             pltpu.VMEM((2, CP * 8, 128), f32),
             pltpu.VMEM((C * 8, AB), f32),
-            pltpu.VMEM((quads, 4, 8, wide), f32),
+            pltpu.VMEM((quads, 4, 8, rows), f32),
             pltpu.SemaphoreType.DMA((21,)),
         ],
         compiler_params=compiler(20),
         name="backward_modes",
-    )(received_back.reshape(quads, 4, 8, rows), high, low, from_hbm(weight), sums)
-    returned_back = exchange(back_cells.reshape(devices, 8, wide))
+    )(received_back.reshape(quads, 4, 8, rows), high, low, from_hbm(weight))
+    returned_back = exchange(back_cells.reshape(devices, 8, rows))
 
     gradient = pl.pallas_call(
         gradient_kernel,
@@ -595,15 +635,11 @@
     )(modes, back_modes)
     spectral_gradient = gradient.reshape(2, MX, MY, C, 4, C).transpose(0, 1, 2, 3, 5, 4)
 
-    features_gradient, pointwise_gradient, bias_gradient = pl.pallas_call(
-        functools.partial(final_kernel, 1.0 / math.sqrt(cells * ZT)),
-        out_shape=(
-            in_hbm((rows, ZT), bf16),
-            jax.ShapeDtypeStruct((C, C), f32),
-            jax.ShapeDtypeStruct((1, C), f32),
-        ),
+    features_gradient = pl.pallas_call(
+        final_kernel,
+        out_shape=in_hbm((rows, ZT), bf16),
         in_specs=[near, near, hbm],
-        out_specs=(hbm, near, near),
+        out_specs=hbm,
         scratch_shapes=[
             pltpu.VMEM((rows, ZT), f32),
             pltpu.VMEM((rows, ZT), bf16),
@@ -611,7 +647,7 @@
         ],
         compiler_params=compiler(16),
         name="features_gradient",
-    )(returned_back, depth, from_hbm(local_back))
+    )(returned_back.reshape(2 * MZT, rows), depth, from_hbm(local_back))
 
     return (
         layer_output.reshape(features.shape),
@@ -762,6 +798,7 @@
         spectral_weight.shape[5] == 4
         and features.shape[1] * features.shape[2] == 32
         and features.shape[3] == ZT
+        and lax.axis_size("gx") * lax.axis_size("gy") == 32
     )
     run = fast_on_device if fits else on_device
     return run(features, spectral_weight, pointwise_weight, pointwise_bias, cotangent)

time: 117 us -> 129 us (1.10)
  blocking collectives: 0 us -> 21.4 us
  waiting for transfers between devices: 34.3 us -> 26.5 us
  Pallas kernels: 62.9 us -> 57.5 us
  starting transfers between devices: 18.4 us -> 22.1 us
    all_to_all x0 -> x1, blocking collectives: none -> 21.4 us  [exchange(): lax.all_to_all(values, ('gx', 'gy'), split_axis=0, concat_axis=0, tiled=T...]
    all_to_all x4 -> x3, waiting for transfers between devices: 34.3 us -> 17.5 us  [exchange(): lax.all_to_all(values, ('gx', 'gy'), split_axis=0, concat_axis=0, tiled=T...]
    ppermute x0 -> x7, waiting for transfers between devices: none -> 9.05 us  [partner(): lax.ppermute(values, ('gx', 'gy'), [(i, i ^ bit) for i in range(devices)])]
    ppermute x0 -> x7, starting transfers between devices: none -> 7.9 us  [partner(): lax.ppermute(values, ('gx', 'gy'), [(i, i ^ bit) for i in range(devices)])]
    all_to_all x4 -> x3, starting transfers between devices: 18.4 us -> 14.2 us  [exchange(): lax.all_to_all(values, ('gx', 'gy'), split_axis=0, concat_axis=0, tiled=T...]
    pallas_call x5 -> x7, Pallas kernels: 21.2 us -> 17.8 us  [the longest x1 4.58 us: fast_on_device(): pl.pallas_call(backward_kernel, out_shape=(in_hbm((quads, 4, 8, rows), f3...]
    pallas_call x1, Pallas kernels: 15 us -> 13 us  [fast_on_device(): pl.pallas_call(weight_kernel, out_shape=in_hbm((2, 4, 2, C, CP, 128), f32...]
  transfers between devices with their start and end apart: 4 -> 10, of which waited for: 4 -> 8; matrix products, arithmetic and copies ran while one was open for 0% -> 0% of each run, Pallas kernels for 34% -> 27%
where the time goes in v3:
time: 129 us; the launch traced here: 128 us
  Pallas kernels  57.5 us (45%)
  waiting for transfers between devices  26.5 us (21%)
  starting transfers between devices  22.1 us (17%)
  blocking collectives  21.4 us (17%)
    all_to_all x1, blocking collectives, exchange(): lax.all_to_all(values, ('gx', 'gy'), split_axis=0, concat_axis=0, tiled=T...  21.4 us
    all_to_all x3, waiting for transfers between devices, exchange(): lax.all_to_all(values, ('gx', 'gy'), split_axis=0, concat_axis=0, tiled=T...  17.5 us
    all_to_all x3, starting transfers between devices, exchange(): lax.all_to_all(values, ('gx', 'gy'), split_axis=0, concat_axis=0, tiled=T...  14.2 us
    pallas_call x1, Pallas kernels, fast_on_device(): pl.pallas_call(weight_kernel, out_shape=in_hbm((2, 4, 2, C, CP, 128), f32...  13 us
    pallas_call x1, Pallas kernels, fast_on_device(): pl.pallas_call(gradient_kernel, out_shape=in_hbm((2, 2, 128 * PAIRS, C),...  11.5 us
    ppermute x7, waiting for transfers between devices, partner(): lax.ppermute(values, ('gx', 'gy'), [(i, i ^ bit) for i in range(devices)])  9.05 us
    ppermute x7, starting transfers between devices, partner(): lax.ppermute(values, ('gx', 'gy'), [(i, i ^ bit) for i in range(devices)])  7.9 us
    pallas_call x1, Pallas kernels, fast_on_device(): pl.pallas_call(layer_kernel, out_shape=(in_hbm((rows, ZT), bf16), in_hbm(...  5.69 us
  transfers between devices with their start and end apart: 10, of which 8 were waited for; matrix products, arithmetic and copies ran while one was open for 0% of the time, Pallas kernels for 27%

profile of v3, /device:TPU:0, one launch (start us, length us, event | category | flops | bytes accessed | tf_op | source)
XLA Modules:
  0.0 128.5 jit_solution(7553461211129544005)
XLA Ops:
  0.6 3.8 %depth.1 = f32[32,8,640]{2,1,0:T(8,128)} custom-call(bf16[256,1024]{1,0:T(8,128)(2,1)} %constant.2.clone.table_hbm.table_ref, bf16[640,1024]{1,0:T(8,128)(2,1)} %bitcast.25), custom_call_target="tpu_custom_call" | custom-call | tf_op jit(solution)/shard_map/depth/pallas_call | solution.py:478
  4.5 7.3 %all-to-all-start = ((f32[32,8,640]{2,1,0:T(8,128)}), f32[32,8,640]{2,1,0:T(8,128)S(1)}, u32[]{:S(2)}, u32[]{:S(2)}) async-start(f32[32,8,640]{2,1,0:T(8,128)} %depth.1), calls=%async_computation | async-start | bytes 1310720 | tf_op jit(solution)/shard_map/all_to_all | solution.py:452
  11.8 13.0 %weights.1.weight_hbm = f32[2,4,2,20,24,128]{5,4,3,2,1,0:T(8,128)} custom-call(f32[2,2,10240,20]{3,2,1,0:T(8,128)} %bitcast.23), custom_call_target="tpu_custom_call" | custom-call | flops 1000000 | bytes 25000000 | tf_op jit(solution)/shard_map/weights/pallas_call | solution.py:495
  24.8 1.1 planes.1
  25.9 3.9 %all-to-all-done = f32[32,8,640]{2,1,0:T(8,128)S(1)} async-done(((f32[32,8,640]{2,1,0:T(8,128)}), f32[32,8,640]{2,1,0:T(8,128)S(1)}, u32[]{:S(2)}, u32[]{:S(2)}) %all-to-all-start) | async-done | bytes 655392 | tf_op jit(solution)/shard_map/all_to_all | solution.py:452
  29.8 4.5 %forward_modes.1 = (f32[8,4,8,640]{3,2,1,0:T(8,128)}, f32[20,8,256]{2,1,0:T(8,128)}) custom-call(f32[8,4,8,640]{3,2,1,0:T(8,128)S(1)} %bitcast.19, bf16[512,1024]{1,0:T(8,128)(2,1)S(1)} %get-tuple-element.18.high_ref, bf16[512,1024]{1,0:T(8,128)(2,1)S(1)} %get-tuple-element.19.low_ref, f32[2,4,2,20,24,128]{5,4,3,2,1,0:T(8,128)} %weights.1.weight_hbm), custom_call_target="tpu_custom_call" | custom-call | tf_op jit(solution)/shard_map/forward_modes/pallas_call | solution.py:522
  34.3 0.0 copy-start
  34.4 3.4 %all-to-all-start.1 = ((f32[32,8,640]{2,1,0:T(8,128)}), f32[32,8,640]{2,1,0:T(8,128)S(1)}, u32[]{:S(2)}, u32[]{:S(2)}) async-start(f32[32,8,640]{2,1,0:T(8,128)} %bitcast.31), calls=%async_computation.1 | async-start | bytes 1310720 | tf_op jit(solution)/shard_map/all_to_all | solution.py:452
  37.8 4.3 %pointwise_ahead.1.local_hbm = f32[640,1024]{1,0:T(8,128)} custom-call(bf16[20,20]{1,0:T(8,128)(2,1)S(1)} %copy-done.3, f32[1,20]{1,0:T(1,128)S(1)} %bitcast.22, bf16[640,1024]{1,0:T(8,128)(2,1)} %bitcast.26), custom_call_target="tpu_custom_call" | custom-call | flops 1000000000 | bytes 5000000 | tf_op jit(solution)/shard_map/pointwise_ahead/pallas_call | solution.py:538
  42.2 13.6 %all-to-all-done.1 = f32[32,8,640]{2,1,0:T(8,128)S(1)} async-done(((f32[32,8,640]{2,1,0:T(8,128)}), f32[32,8,640]{2,1,0:T(8,128)S(1)}, u32[]{:S(2)}, u32[]{:S(2)}) %all-to-all-start.1) | async-done | bytes 655392 | tf_op jit(solution)/shard_map/all_to_all | solution.py:452
  55.8 5.7 %layer.1 = (bf16[640,1024]{1,0:T(8,128)(2,1)}, bf16[640,1024]{1,0:T(8,128)(2,1)}, f32[32,8,640]{2,1,0:T(8,128)}) custom-call(f32[256,640]{1,0:T(8,128)S(1)} %bitcast.20, bf16[256,1024]{1,0:T(8,128)(2,1)S(1)} %copy-done, f32[640,1024]{1,0:T(8,128)} %pointwise_ahead.1.local_hbm, bf16[640,1024]{1,0:T(8,128)(2,1)} %bitcast.28), custom_call_target="tpu_custom_call" | custom-call | tf_op jit(solution)/shard_map/layer/pallas_call | solution.py:547
  61.5 21.4 %all_to_all.20 = f32[32,8,640]{2,1,0:T(8,128)S(1)} all-to-all(f32[32,8,640]{2,1,0:T(8,128)} %get-tuple-element.22), channel_id=1, replica_groups=mesh['gx'=8,'gy'=4] {'gx','gy'}, dimensions={0} | all-to-all | bytes 1310720 | tf_op jit(solution)/shard_map/all_to_all | solution.py:452
  82.9 4.6 %backward_modes.1 = (f32[8,4,8,640]{3,2,1,0:T(8,128)}, f32[20,8,256]{2,1,0:T(8,128)}) custom-call(f32[8,4,8,640]{3,2,1,0:T(8,128)S(1)} %bitcast.21, bf16[512,1024]{1,0:T(8,128)(2,1)S(1)} %get-tuple-element.18.high_ref, bf16[512,1024]{1,0:T(8,128)(2,1)S(1)} %get-tuple-element.19.low_ref, f32[2,4,2,20,24,128]{5,4,3,2,1,0:T(8,128)} %weights.1.weight_hbm), custom_call_target="tpu_custom_call" | custom-call | tf_op jit(solution)/shard_map/backward_modes/pallas_call | solution.py:605
  87.5 3.4 %all-to-all-start.3 = ((f32[32,8,640]{2,1,0:T(8,128)}), f32[32,8,640]{2,1,0:T(8,128)S(1)}, u32[]{:S(2)}, u32[]{:S(2)}) async-start(f32[32,8,640]{2,1,0:T(8,128)} %bitcast.30), calls=%async_computation.3 | async-start | bytes 1310720 | tf_op jit(solution)/shard_map/all_to_all | solution.py:452
  90.9 4.6 %products.1 = (f32[8,128]{1,0:T(8,128)S(1)}, f32[640,1024]{1,0:T(8,128)}) custom-call(bf16[20,20]{1,0:T(8,128)(2,1)S(1)} %copy-done.3, bf16[640,1024]{1,0:T(8,128)(2,1)} %bitcast.27, bf16[640,1024]{1,0:T(8,128)(2,1)} %get-tuple-element.24.gradient_hbm), custom_call_target="tpu_custom_call" | custom-call | flops 2000000000 | bytes 6000000 | tf_op jit(solution)/shard_map/products/pallas_call | solution.py:569
  95.5 0.3 collective-permute-start
  95.8 1.6 %collective-permute-start.1 = (f32[8,128]{1,0:T(8,128)S(1)}, f32[8,128]{1,0:T(8,128)S(1)}, u32[]{:S(2)}, u32[]{:S(2)}) collective-permute-start(f32[8,128]{1,0:T(8,128)S(1)} %get-tuple-element.28.own_ref), channel_id=1, source_target_pairs={{0,2},{1,3},{2,0},{3,1},{4,6},{5,7},{6,4},{7,5},{8,10},{9,11},{10,... | collective-permute-start | bytes 12296 | tf_op jit(solution)/shard_map/ppermute | solution.py:456
  97.4 0.0 collective-permute-start.2
  97.5 2.2 %collective-permute-done.1.second_ref = f32[8,128]{1,0:T(8,128)S(1)} collective-permute-done((f32[8,128]{1,0:T(8,128)S(1)}, f32[8,128]{1,0:T(8,128)S(1)}, u32[]{:S(2)}, u32[]{:S(2)}) %collective-permute-start.1) | collective-permute-done | bytes 4128 | tf_op jit(solution)/shard_map/ppermute | solution.py:456
  99.7 0.9 collective-permute-done.2.third_ref
  100.5 1.4 %collective-permute-start.3 = (f32[8,128]{1,0:T(8,128)S(1)}, f32[8,128]{1,0:T(8,128)S(1)}, u32[]{:S(2)}, u32[]{:S(2)}) collective-permute-start(f32[8,128]{1,0:T(8,128)S(1)} %quad_sum.2.own_ref), channel_id=1, source_target_pairs={{0,4},{1,5},{2,6},{3,7},{4,0},{5,1},{6,2},{7,3},{8,12},{9,13},{10,... | collective-permute-start | bytes 12296 | tf_op jit(solution)/shard_map/ppermute | solution.py:456
  101.9 1.5 %collective-permute-start.4 = (f32[8,128]{1,0:T(8,128)S(1)}, f32[8,128]{1,0:T(8,128)S(1)}, u32[]{:S(2)}, u32[]{:S(2)}) collective-permute-start(f32[8,128]{1,0:T(8,128)S(1)} %quad_sum.2.own_ref), channel_id=1, source_target_pairs={{0,8},{1,9},{2,10},{3,11},{4,12},{5,13},{6,14},{7,15},{8,0},{9,1},... | collective-permute-start | bytes 12296 | tf_op jit(solution)/shard_map/ppermute | solution.py:456
  103.4 0.6 collective-permute-start.5
  104.0 0.1 collective-permute-done.3.first_ref
  104.1 1.6 %collective-permute-done.4.second_ref = f32[8,128]{1,0:T(8,128)S(1)} collective-permute-done((f32[8,128]{1,0:T(8,128)S(1)}, f32[8,128]{1,0:T(8,128)S(1)}, u32[]{:S(2)}, u32[]{:S(2)}) %collective-permute-start.4) | collective-permute-done | bytes 4128 | tf_op jit(solution)/shard_map/ppermute | solution.py:456
  105.7 2.2 %collective-permute-done.5.third_ref = f32[8,128]{1,0:T(8,128)S(1)} collective-permute-done((f32[8,128]{1,0:T(8,128)S(1)}, f32[8,128]{1,0:T(8,128)S(1)}, u32[]{:S(2)}, u32[]{:S(2)}) %collective-permute-start.5) | collective-permute-done | bytes 4128 | tf_op jit(solution)/shard_map/ppermute | solution.py:456
  107.9 2.5 %collective-permute-start.6 = (f32[8,128]{1,0:T(8,128)S(1)}, f32[8,128]{1,0:T(8,128)S(1)}, u32[]{:S(2)}, u32[]{:S(2)}) collective-permute-start(f32[8,128]{1,0:T(8,128)S(1)} %quad_sum.3.own_ref), channel_id=1, source_target_pairs={{0,16},{1,17},{2,18},{3,19},{4,20},{5,21},{6,22},{7,23},{8,24},{9,... | collective-permute-start | bytes 12296 | tf_op jit(solution)/shard_map/ppermute | solution.py:456
  110.4 2.1 %collective-permute-done.6.other_ref = f32[8,128]{1,0:T(8,128)S(1)} collective-permute-done((f32[8,128]{1,0:T(8,128)S(1)}, f32[8,128]{1,0:T(8,128)S(1)}, u32[]{:S(2)}, u32[]{:S(2)}) %collective-permute-start.6) | collective-permute-done | bytes 4128 | tf_op jit(solution)/shard_map/ppermute | solution.py:456
  112.5 0.7 total_sum.1
  113.1 11.5 %spectral_gradient.1 = f32[2,2,10240,20]{3,2,1,0:T(8,128)} custom-call(f32[20,8,256]{2,1,0:T(8,128)S(1)} %copy-done.1, f32[20,8,256]{2,1,0:T(8,128)S(1)} %copy-done.2), custom_call_target="tpu_custom_call" | custom-call | flops 1000000 | bytes 25000000 | tf_op jit(solution)/shard_map/spectral_gradient/pallas_call | solution.py:622
  124.6 0.0 all-to-all-done.3
  124.6 3.7 %features_gradient.1 = bf16[640,1024]{1,0:T(8,128)(2,1)} custom-call(f32[256,640]{1,0:T(8,128)S(1)} %bitcast.18, bf16[256,1024]{1,0:T(8,128)(2,1)S(1)} %copy-done, f32[640,1024]{1,0:T(8,128)} %get-tuple-element.25.local_hbm), custom_call_target="tpu_custom_call" | custom-call | tf_op jit(solution)/shard_map/features_gradient/pallas_call | solution.py:638
  (12 shorter events, 0.0 us)
Async XLA Ops:
  4.5 25.3 %all-to-all-start = ((f32[32,8,640]{2,1,0:T(8,128)}), f32[32,8,640]{2,1,0:T(8,128)S(1)}, u32[]{:S(2)}, u32[]{:S(2)}) async-start(f32[32,8,640]{2,1,0:T(8,128)} %depth.1), calls=%async_computation | async-start | bytes 1310720 | tf_op jit(solution)/shard_map/all_to_all | solution.py:452
  29.8 8.0 %copy-start.3 = (bf16[20,20]{1,0:T(8,128)(2,1)S(1)}, bf16[20,20]{1,0:T(8,128)(2,1)}, u32[]{:S(2)}) copy-start(bf16[20,20]{1,0:T(8,128)(2,1)} %weight_ref.3) | copy-start | bytes 2404
  29.8 8.0 %copy-start.4 = (f32[20]{0:T(128)S(1)}, f32[20]{0:T(128)}, u32[]{:S(2)}) copy-start(f32[20]{0:T(128)} %param.9) | copy-start | bytes 244
  34.3 21.4 %copy-start = (bf16[256,1024]{1,0:T(8,128)(2,1)S(1)}, bf16[256,1024]{1,0:T(8,128)(2,1)}, u32[]{:S(2)}) copy-start(bf16[256,1024]{1,0:T(8,128)(2,1)} %constant.2.clone.table_hbm.table_ref) | copy-start | bytes 1572868
  34.4 21.4 %all-to-all-start.1 = ((f32[32,8,640]{2,1,0:T(8,128)}), f32[32,8,640]{2,1,0:T(8,128)S(1)}, u32[]{:S(2)}, u32[]{:S(2)}) async-start(f32[32,8,640]{2,1,0:T(8,128)} %bitcast.31), calls=%async_computation.1 | async-start | bytes 1310720 | tf_op jit(solution)/shard_map/all_to_all | solution.py:452
  87.5 37.2 %all-to-all-start.3 = ((f32[32,8,640]{2,1,0:T(8,128)}), f32[32,8,640]{2,1,0:T(8,128)S(1)}, u32[]{:S(2)}, u32[]{:S(2)}) async-start(f32[32,8,640]{2,1,0:T(8,128)} %bitcast.30), calls=%async_computation.3 | async-start | bytes 1310720 | tf_op jit(solution)/shard_map/all_to_all | solution.py:452
  90.9 22.2 %copy-start.1 = (f32[20,8,256]{2,1,0:T(8,128)S(1)}, f32[20,8,256]{2,1,0:T(8,128)}, u32[]{:S(2)}) copy-start(f32[20,8,256]{2,1,0:T(8,128)} %get-tuple-element.26.forward_ref) | copy-start | bytes 491524
  90.9 22.2 %copy-start.2 = (f32[20,8,256]{2,1,0:T(8,128)S(1)}, f32[20,8,256]{2,1,0:T(8,128)}, u32[]{:S(2)}) copy-start(f32[20,8,256]{2,1,0:T(8,128)} %get-tuple-element.27.backward_ref) | copy-start | bytes 491524
  95.5 2.0 %collective-permute-start = (f32[8,128]{1,0:T(8,128)S(1)}, f32[8,128]{1,0:T(8,128)S(1)}, u32[]{:S(2)}, u32[]{:S(2)}) collective-permute-start(f32[8,128]{1,0:T(8,128)S(1)} %get-tuple-element.28.own_ref), channel_id=1, source_target_pairs={{0,1},{1,0},{2,3},{3,2},{4,5},{5,4},{6,7},{7,6},{8,9},{9,8},{10,11... | collective-permute-start | bytes 12296 | tf_op jit(solution)/shard_map/ppermute | solution.py:456
  95.8 3.9 %collective-permute-start.1 = (f32[8,128]{1,0:T(8,128)S(1)}, f32[8,128]{1,0:T(8,128)S(1)}, u32[]{:S(2)}, u32[]{:S(2)}) collective-permute-start(f32[8,128]{1,0:T(8,128)S(1)} %get-tuple-element.28.own_ref), channel_id=1, source_target_pairs={{0,2},{1,3},{2,0},{3,1},{4,6},{5,7},{6,4},{7,5},{8,10},{9,11},{10,... | collective-permute-start | bytes 12296 | tf_op jit(solution)/shard_map/ppermute | solution.py:456
  97.4 3.1 %collective-permute-start.2 = (f32[8,128]{1,0:T(8,128)S(1)}, f32[8,128]{1,0:T(8,128)S(1)}, u32[]{:S(2)}, u32[]{:S(2)}) collective-permute-start(f32[8,128]{1,0:T(8,128)S(1)} %get-tuple-element.28.own_ref), channel_id=1, source_target_pairs={{0,3},{1,2},{2,1},{3,0},{4,7},{5,6},{6,5},{7,4},{8,11},{9,10},{10,... | collective-permute-start | bytes 12296 | tf_op jit(solution)/shard_map/ppermute | solution.py:456
  100.5 3.6 %collective-permute-start.3 = (f32[8,128]{1,0:T(8,128)S(1)}, f32[8,128]{1,0:T(8,128)S(1)}, u32[]{:S(2)}, u32[]{:S(2)}) collective-permute-start(f32[8,128]{1,0:T(8,128)S(1)} %quad_sum.2.own_ref), channel_id=1, source_target_pairs={{0,4},{1,5},{2,6},{3,7},{4,0},{5,1},{6,2},{7,3},{8,12},{9,13},{10,... | collective-permute-start | bytes 12296 | tf_op jit(solution)/shard_map/ppermute | solution.py:456
  101.9 3.8 %collective-permute-start.4 = (f32[8,128]{1,0:T(8,128)S(1)}, f32[8,128]{1,0:T(8,128)S(1)}, u32[]{:S(2)}, u32[]{:S(2)}) collective-permute-start(f32[8,128]{1,0:T(8,128)S(1)} %quad_sum.2.own_ref), channel_id=1, source_target_pairs={{0,8},{1,9},{2,10},{3,11},{4,12},{5,13},{6,14},{7,15},{8,0},{9,1},... | collective-permute-start | bytes 12296 | tf_op jit(solution)/shard_map/ppermute | solution.py:456
  103.4 4.5 %collective-permute-start.5 = (f32[8,128]{1,0:T(8,128)S(1)}, f32[8,128]{1,0:T(8,128)S(1)}, u32[]{:S(2)}, u32[]{:S(2)}) collective-permute-start(f32[8,128]{1,0:T(8,128)S(1)} %quad_sum.2.own_ref), channel_id=1, source_target_pairs={{0,12},{1,13},{2,14},{3,15},{4,8},{5,9},{6,10},{7,11},{8,4},{9,5},... | collective-permute-start | bytes 12296 | tf_op jit(solution)/shard_map/ppermute | solution.py:456
  107.9 4.5 %collective-permute-start.6 = (f32[8,128]{1,0:T(8,128)S(1)}, f32[8,128]{1,0:T(8,128)S(1)}, u32[]{:S(2)}, u32[]{:S(2)}) collective-permute-start(f32[8,128]{1,0:T(8,128)S(1)} %quad_sum.3.own_ref), channel_id=1, source_target_pairs={{0,16},{1,17},{2,18},{3,19},{4,20},{5,21},{6,22},{7,23},{8,24},{9,... | collective-permute-start | bytes 12296 | tf_op jit(solution)/shard_map/ppermute | solution.py:456

commit v4 on v3

--- a/solution.py
+++ b/solution.py
@@ -330,12 +330,12 @@
         cotangent_copies.append(
             start(cotangent_hbm.at[:, lanes], cotangent_ref.at[:, lanes], sems.at[6 + s])
         )
-    high, low = split(recv_ref[...].T)
+    high = recv_ref[...].astype(bf16).T
     total = None
     copies = []
     for s, lanes in enumerate(columns):
         table = table_ref[:, lanes]
-        spectral = dot(high, table, NN) + dot(low, table, NN)
+        spectral = dot(high, table, NN)
         local_copies[s].wait()
         activated, slopes = activation(spectral + local_ref[:, lanes])
         out_ref[:, lanes] = activated.astype(bf16)
@@ -404,11 +404,11 @@
         start(local_hbm.at[:, lanes], local_ref.at[:, lanes], sems.at[2 + s])
         for s, lanes in enumerate(columns)
     ]
-    high, low = split(recv_ref[...].T)
+    high = recv_ref[...].astype(bf16).T
     copies = []
     for s, lanes in enumerate(columns):
         table = table_ref[:, lanes]
-        spectral = dot(high, table, NN) + dot(low, table, NN)
+        spectral = dot(high, table, NN)
         local_copies[s].wait()
         out_ref[:, lanes] = (spectral + local_ref[:, lanes]).astype(bf16)
         copies.append(start(out_ref.at[:, lanes], out_hbm.at[:, lanes], sems.at[6 + s]))

time: 129 us -> 128 us (level)
  transfers between devices with their start and end apart: 10 -> 10, of which waited for: 8 -> 8; matrix products, arithmetic and copies ran while one was open for 0% -> 0% of each run, Pallas kernels for 27% -> 28%
where the time goes in v4:
time: 128 us; the launch traced here: 127 us
  Pallas kernels  56.4 us (44%)
  waiting for transfers between devices  26.5 us (21%)
  starting transfers between devices  22.1 us (17%)
  blocking collectives  21.4 us (17%)
    all_to_all x1, blocking collectives, exchange(): lax.all_to_all(values, ('gx', 'gy'), split_axis=0, concat_axis=0, tiled=T...  21.4 us
    all_to_all x3, waiting for transfers between devices, exchange(): lax.all_to_all(values, ('gx', 'gy'), split_axis=0, concat_axis=0, tiled=T...  17.5 us
    all_to_all x3, starting transfers between devices, exchange(): lax.all_to_all(values, ('gx', 'gy'), split_axis=0, concat_axis=0, tiled=T...  14.2 us
    pallas_call x1, Pallas kernels, fast_on_device(): pl.pallas_call(weight_kernel, out_shape=in_hbm((2, 4, 2, C, CP, 128), f32...  13 us
    pallas_call x1, Pallas kernels, fast_on_device(): pl.pallas_call(gradient_kernel, out_shape=in_hbm((2, 2, 128 * PAIRS, C),...  11.5 us
    ppermute x7, waiting for transfers between devices, partner(): lax.ppermute(values, ('gx', 'gy'), [(i, i ^ bit) for i in range(devices)])  9.07 us
    ppermute x7, starting transfers between devices, partner(): lax.ppermute(values, ('gx', 'gy'), [(i, i ^ bit) for i in range(devices)])  7.89 us
    pallas_call x1, Pallas kernels, fast_on_device(): pl.pallas_call(layer_kernel, out_shape=(in_hbm((rows, ZT), bf16), in_hbm(...  4.99 us
  transfers between devices with their start and end apart: 10, of which 8 were waited for; matrix products, arithmetic and copies ran while one was open for 0% of the time, Pallas kernels for 28%

profile of v4, /device:TPU:0, one launch (start us, length us, event | category | flops | bytes accessed | tf_op | source)
XLA Modules:
  0.0 127.3 jit_solution(13774967547036010319)
XLA Ops:
  0.6 3.8 %depth.1 = f32[32,8,640]{2,1,0:T(8,128)} custom-call(bf16[256,1024]{1,0:T(8,128)(2,1)} %constant.2.clone.table_hbm.table_ref, bf16[640,1024]{1,0:T(8,128)(2,1)} %bitcast.25), custom_call_target="tpu_custom_call" | custom-call | tf_op jit(solution)/shard_map/depth/pallas_call | solution.py:478
  4.5 7.3 %all-to-all-start = ((f32[32,8,640]{2,1,0:T(8,128)}), f32[32,8,640]{2,1,0:T(8,128)S(1)}, u32[]{:S(2)}, u32[]{:S(2)}) async-start(f32[32,8,640]{2,1,0:T(8,128)} %depth.1), calls=%async_computation | async-start | bytes 1310720 | tf_op jit(solution)/shard_map/all_to_all | solution.py:452
  11.8 13.0 %weights.1.weight_hbm = f32[2,4,2,20,24,128]{5,4,3,2,1,0:T(8,128)} custom-call(f32[2,2,10240,20]{3,2,1,0:T(8,128)} %bitcast.23), custom_call_target="tpu_custom_call" | custom-call | flops 1000000 | bytes 25000000 | tf_op jit(solution)/shard_map/weights/pallas_call | solution.py:495
  24.8 1.1 planes.1
  25.9 3.9 %all-to-all-done = f32[32,8,640]{2,1,0:T(8,128)S(1)} async-done(((f32[32,8,640]{2,1,0:T(8,128)}), f32[32,8,640]{2,1,0:T(8,128)S(1)}, u32[]{:S(2)}, u32[]{:S(2)}) %all-to-all-start) | async-done | bytes 655392 | tf_op jit(solution)/shard_map/all_to_all | solution.py:452
  29.8 4.5 %forward_modes.1 = (f32[8,4,8,640]{3,2,1,0:T(8,128)}, f32[20,8,256]{2,1,0:T(8,128)}) custom-call(f32[8,4,8,640]{3,2,1,0:T(8,128)S(1)} %bitcast.19, bf16[512,1024]{1,0:T(8,128)(2,1)S(1)} %get-tuple-element.18.high_ref, bf16[512,1024]{1,0:T(8,128)(2,1)S(1)} %get-tuple-element.19.low_ref, f32[2,4,2,20,24,128]{5,4,3,2,1,0:T(8,128)} %weights.1.weight_hbm), custom_call_target="tpu_custom_call" | custom-call | tf_op jit(solution)/shard_map/forward_modes/pallas_call | solution.py:522
  34.3 0.0 copy-start
  34.4 3.4 %all-to-all-start.1 = ((f32[32,8,640]{2,1,0:T(8,128)}), f32[32,8,640]{2,1,0:T(8,128)S(1)}, u32[]{:S(2)}, u32[]{:S(2)}) async-start(f32[32,8,640]{2,1,0:T(8,128)} %bitcast.31), calls=%async_computation.1 | async-start | bytes 1310720 | tf_op jit(solution)/shard_map/all_to_all | solution.py:452
  37.8 4.3 %pointwise_ahead.1.local_hbm = f32[640,1024]{1,0:T(8,128)} custom-call(bf16[20,20]{1,0:T(8,128)(2,1)S(1)} %copy-done.3, f32[1,20]{1,0:T(1,128)S(1)} %bitcast.22, bf16[640,1024]{1,0:T(8,128)(2,1)} %bitcast.26), custom_call_target="tpu_custom_call" | custom-call | flops 1000000000 | bytes 5000000 | tf_op jit(solution)/shard_map/pointwise_ahead/pallas_call | solution.py:538
  42.2 13.6 %all-to-all-done.1 = f32[32,8,640]{2,1,0:T(8,128)S(1)} async-done(((f32[32,8,640]{2,1,0:T(8,128)}), f32[32,8,640]{2,1,0:T(8,128)S(1)}, u32[]{:S(2)}, u32[]{:S(2)}) %all-to-all-start.1) | async-done | bytes 655392 | tf_op jit(solution)/shard_map/all_to_all | solution.py:452
  55.8 5.0 %layer.1 = (bf16[640,1024]{1,0:T(8,128)(2,1)}, bf16[640,1024]{1,0:T(8,128)(2,1)}, f32[32,8,640]{2,1,0:T(8,128)}) custom-call(f32[256,640]{1,0:T(8,128)S(1)} %bitcast.20, bf16[256,1024]{1,0:T(8,128)(2,1)S(1)} %copy-done, f32[640,1024]{1,0:T(8,128)} %pointwise_ahead.1.local_hbm, bf16[640,1024]{1,0:T(8,128)(2,1)} %bitcast.28), custom_call_target="tpu_custom_call" | custom-call | tf_op jit(solution)/shard_map/layer/pallas_call | solution.py:547
  60.8 21.4 %all_to_all.20 = f32[32,8,640]{2,1,0:T(8,128)S(1)} all-to-all(f32[32,8,640]{2,1,0:T(8,128)} %get-tuple-element.22), channel_id=1, replica_groups=mesh['gx'=8,'gy'=4] {'gx','gy'}, dimensions={0} | all-to-all | bytes 1310720 | tf_op jit(solution)/shard_map/all_to_all | solution.py:452
  82.2 4.6 %backward_modes.1 = (f32[8,4,8,640]{3,2,1,0:T(8,128)}, f32[20,8,256]{2,1,0:T(8,128)}) custom-call(f32[8,4,8,640]{3,2,1,0:T(8,128)S(1)} %bitcast.21, bf16[512,1024]{1,0:T(8,128)(2,1)S(1)} %get-tuple-element.18.high_ref, bf16[512,1024]{1,0:T(8,128)(2,1)S(1)} %get-tuple-element.19.low_ref, f32[2,4,2,20,24,128]{5,4,3,2,1,0:T(8,128)} %weights.1.weight_hbm), custom_call_target="tpu_custom_call" | custom-call | tf_op jit(solution)/shard_map/backward_modes/pallas_call | solution.py:605
  86.8 3.4 %all-to-all-start.3 = ((f32[32,8,640]{2,1,0:T(8,128)}), f32[32,8,640]{2,1,0:T(8,128)S(1)}, u32[]{:S(2)}, u32[]{:S(2)}) async-start(f32[32,8,640]{2,1,0:T(8,128)} %bitcast.30), calls=%async_computation.3 | async-start | bytes 1310720 | tf_op jit(solution)/shard_map/all_to_all | solution.py:452
  90.2 4.6 %products.1 = (f32[8,128]{1,0:T(8,128)S(1)}, f32[640,1024]{1,0:T(8,128)}) custom-call(bf16[20,20]{1,0:T(8,128)(2,1)S(1)} %copy-done.3, bf16[640,1024]{1,0:T(8,128)(2,1)} %bitcast.27, bf16[640,1024]{1,0:T(8,128)(2,1)} %get-tuple-element.24.gradient_hbm), custom_call_target="tpu_custom_call" | custom-call | flops 2000000000 | bytes 6000000 | tf_op jit(solution)/shard_map/products/pallas_call | solution.py:569
  94.8 0.3 collective-permute-start
  95.1 1.6 %collective-permute-start.1 = (f32[8,128]{1,0:T(8,128)S(1)}, f32[8,128]{1,0:T(8,128)S(1)}, u32[]{:S(2)}, u32[]{:S(2)}) collective-permute-start(f32[8,128]{1,0:T(8,128)S(1)} %get-tuple-element.28.own_ref), channel_id=1, source_target_pairs={{0,2},{1,3},{2,0},{3,1},{4,6},{5,7},{6,4},{7,5},{8,10},{9,11},{10,... | collective-permute-start | bytes 12296 | tf_op jit(solution)/shard_map/ppermute | solution.py:456
  96.8 0.0 collective-permute-start.2
  96.8 0.0 collective-permute-done.first_ref
  96.8 2.2 %collective-permute-done.1.second_ref = f32[8,128]{1,0:T(8,128)S(1)} collective-permute-done((f32[8,128]{1,0:T(8,128)S(1)}, f32[8,128]{1,0:T(8,128)S(1)}, u32[]{:S(2)}, u32[]{:S(2)}) %collective-permute-start.1) | collective-permute-done | bytes 4128 | tf_op jit(solution)/shard_map/ppermute | solution.py:456
  99.0 0.9 collective-permute-done.2.third_ref
  99.8 1.4 %collective-permute-start.3 = (f32[8,128]{1,0:T(8,128)S(1)}, f32[8,128]{1,0:T(8,128)S(1)}, u32[]{:S(2)}, u32[]{:S(2)}) collective-permute-start(f32[8,128]{1,0:T(8,128)S(1)} %quad_sum.2.own_ref), channel_id=1, source_target_pairs={{0,4},{1,5},{2,6},{3,7},{4,0},{5,1},{6,2},{7,3},{8,12},{9,13},{10,... | collective-permute-start | bytes 12296 | tf_op jit(solution)/shard_map/ppermute | solution.py:456
  101.3 1.5 %collective-permute-start.4 = (f32[8,128]{1,0:T(8,128)S(1)}, f32[8,128]{1,0:T(8,128)S(1)}, u32[]{:S(2)}, u32[]{:S(2)}) collective-permute-start(f32[8,128]{1,0:T(8,128)S(1)} %quad_sum.2.own_ref), channel_id=1, source_target_pairs={{0,8},{1,9},{2,10},{3,11},{4,12},{5,13},{6,14},{7,15},{8,0},{9,1},... | collective-permute-start | bytes 12296 | tf_op jit(solution)/shard_map/ppermute | solution.py:456
  102.7 0.6 collective-permute-start.5
  103.3 0.1 collective-permute-done.3.first_ref
  103.4 1.6 %collective-permute-done.4.second_ref = f32[8,128]{1,0:T(8,128)S(1)} collective-permute-done((f32[8,128]{1,0:T(8,128)S(1)}, f32[8,128]{1,0:T(8,128)S(1)}, u32[]{:S(2)}, u32[]{:S(2)}) %collective-permute-start.4) | collective-permute-done | bytes 4128 | tf_op jit(solution)/shard_map/ppermute | solution.py:456
  105.0 2.2 %collective-permute-done.5.third_ref = f32[8,128]{1,0:T(8,128)S(1)} collective-permute-done((f32[8,128]{1,0:T(8,128)S(1)}, f32[8,128]{1,0:T(8,128)S(1)}, u32[]{:S(2)}, u32[]{:S(2)}) %collective-permute-start.5) | collective-permute-done | bytes 4128 | tf_op jit(solution)/shard_map/ppermute | solution.py:456
  107.3 2.4 %collective-permute-start.6 = (f32[8,128]{1,0:T(8,128)S(1)}, f32[8,128]{1,0:T(8,128)S(1)}, u32[]{:S(2)}, u32[]{:S(2)}) collective-permute-start(f32[8,128]{1,0:T(8,128)S(1)} %quad_sum.3.own_ref), channel_id=1, source_target_pairs={{0,16},{1,17},{2,18},{3,19},{4,20},{5,21},{6,22},{7,23},{8,24},{9,... | collective-permute-start | bytes 12296 | tf_op jit(solution)/shard_map/ppermute | solution.py:456
  109.7 2.1 %collective-permute-done.6.other_ref = f32[8,128]{1,0:T(8,128)S(1)} collective-permute-done((f32[8,128]{1,0:T(8,128)S(1)}, f32[8,128]{1,0:T(8,128)S(1)}, u32[]{:S(2)}, u32[]{:S(2)}) %collective-permute-start.6) | collective-permute-done | bytes 4128 | tf_op jit(solution)/shard_map/ppermute | solution.py:456
  111.8 0.7 total_sum.1
  112.5 11.5 %spectral_gradient.1 = f32[2,2,10240,20]{3,2,1,0:T(8,128)} custom-call(f32[20,8,256]{2,1,0:T(8,128)S(1)} %copy-done.1, f32[20,8,256]{2,1,0:T(8,128)S(1)} %copy-done.2), custom_call_target="tpu_custom_call" | custom-call | flops 1000000 | bytes 25000000 | tf_op jit(solution)/shard_map/spectral_gradient/pallas_call | solution.py:622
  124.0 3.2 %features_gradient.1 = bf16[640,1024]{1,0:T(8,128)(2,1)} custom-call(f32[256,640]{1,0:T(8,128)S(1)} %bitcast.18, bf16[256,1024]{1,0:T(8,128)(2,1)S(1)} %copy-done, f32[640,1024]{1,0:T(8,128)} %get-tuple-element.25.local_hbm), custom_call_target="tpu_custom_call" | custom-call | tf_op jit(solution)/shard_map/features_gradient/pallas_call | solution.py:638
  (12 shorter events, 0.0 us)
Async XLA Ops:
  4.5 25.3 %all-to-all-start = ((f32[32,8,640]{2,1,0:T(8,128)}), f32[32,8,640]{2,1,0:T(8,128)S(1)}, u32[]{:S(2)}, u32[]{:S(2)}) async-start(f32[32,8,640]{2,1,0:T(8,128)} %depth.1), calls=%async_computation | async-start | bytes 1310720 | tf_op jit(solution)/shard_map/all_to_all | solution.py:452
  29.8 8.0 %copy-start.3 = (bf16[20,20]{1,0:T(8,128)(2,1)S(1)}, bf16[20,20]{1,0:T(8,128)(2,1)}, u32[]{:S(2)}) copy-start(bf16[20,20]{1,0:T(8,128)(2,1)} %weight_ref.3) | copy-start | bytes 2404
  29.8 8.0 %copy-start.4 = (f32[20]{0:T(128)S(1)}, f32[20]{0:T(128)}, u32[]{:S(2)}) copy-start(f32[20]{0:T(128)} %param.9) | copy-start | bytes 244
  34.3 21.4 %copy-start = (bf16[256,1024]{1,0:T(8,128)(2,1)S(1)}, bf16[256,1024]{1,0:T(8,128)(2,1)}, u32[]{:S(2)}) copy-start(bf16[256,1024]{1,0:T(8,128)(2,1)} %constant.2.clone.table_hbm.table_ref) | copy-start | bytes 1572868
  34.4 21.4 %all-to-all-start.1 = ((f32[32,8,640]{2,1,0:T(8,128)}), f32[32,8,640]{2,1,0:T(8,128)S(1)}, u32[]{:S(2)}, u32[]{:S(2)}) async-start(f32[32,8,640]{2,1,0:T(8,128)} %bitcast.31), calls=%async_computation.1 | async-start | bytes 1310720 | tf_op jit(solution)/shard_map/all_to_all | solution.py:452
  86.8 37.2 %all-to-all-start.3 = ((f32[32,8,640]{2,1,0:T(8,128)}), f32[32,8,640]{2,1,0:T(8,128)S(1)}, u32[]{:S(2)}, u32[]{:S(2)}) async-start(f32[32,8,640]{2,1,0:T(8,128)} %bitcast.30), calls=%async_computation.3 | async-start | bytes 1310720 | tf_op jit(solution)/shard_map/all_to_all | solution.py:452
  90.2 22.2 %copy-start.1 = (f32[20,8,256]{2,1,0:T(8,128)S(1)}, f32[20,8,256]{2,1,0:T(8,128)}, u32[]{:S(2)}) copy-start(f32[20,8,256]{2,1,0:T(8,128)} %get-tuple-element.26.forward_ref) | copy-start | bytes 491524
  90.2 22.2 %copy-start.2 = (f32[20,8,256]{2,1,0:T(8,128)S(1)}, f32[20,8,256]{2,1,0:T(8,128)}, u32[]{:S(2)}) copy-start(f32[20,8,256]{2,1,0:T(8,128)} %get-tuple-element.27.backward_ref) | copy-start | bytes 491524
  94.8 2.0 %collective-permute-start = (f32[8,128]{1,0:T(8,128)S(1)}, f32[8,128]{1,0:T(8,128)S(1)}, u32[]{:S(2)}, u32[]{:S(2)}) collective-permute-start(f32[8,128]{1,0:T(8,128)S(1)} %get-tuple-element.28.own_ref), channel_id=1, source_target_pairs={{0,1},{1,0},{2,3},{3,2},{4,5},{5,4},{6,7},{7,6},{8,9},{9,8},{10,11... | collective-permute-start | bytes 12296 | tf_op jit(solution)/shard_map/ppermute | solution.py:456
  95.1 3.8 %collective-permute-start.1 = (f32[8,128]{1,0:T(8,128)S(1)}, f32[8,128]{1,0:T(8,128)S(1)}, u32[]{:S(2)}, u32[]{:S(2)}) collective-permute-start(f32[8,128]{1,0:T(8,128)S(1)} %get-tuple-element.28.own_ref), channel_id=1, source_target_pairs={{0,2},{1,3},{2,0},{3,1},{4,6},{5,7},{6,4},{7,5},{8,10},{9,11},{10,... | collective-permute-start | bytes 12296 | tf_op jit(solution)/shard_map/ppermute | solution.py:456
  96.8 3.1 %collective-permute-start.2 = (f32[8,128]{1,0:T(8,128)S(1)}, f32[8,128]{1,0:T(8,128)S(1)}, u32[]{:S(2)}, u32[]{:S(2)}) collective-permute-start(f32[8,128]{1,0:T(8,128)S(1)} %get-tuple-element.28.own_ref), channel_id=1, source_target_pairs={{0,3},{1,2},{2,1},{3,0},{4,7},{5,6},{6,5},{7,4},{8,11},{9,10},{10,... | collective-permute-start | bytes 12296 | tf_op jit(solution)/shard_map/ppermute | solution.py:456
  99.8 3.6 %collective-permute-start.3 = (f32[8,128]{1,0:T(8,128)S(1)}, f32[8,128]{1,0:T(8,128)S(1)}, u32[]{:S(2)}, u32[]{:S(2)}) collective-permute-start(f32[8,128]{1,0:T(8,128)S(1)} %quad_sum.2.own_ref), channel_id=1, source_target_pairs={{0,4},{1,5},{2,6},{3,7},{4,0},{5,1},{6,2},{7,3},{8,12},{9,13},{10,... | collective-permute-start | bytes 12296 | tf_op jit(solution)/shard_map/ppermute | solution.py:456
  101.3 3.8 %collective-permute-start.4 = (f32[8,128]{1,0:T(8,128)S(1)}, f32[8,128]{1,0:T(8,128)S(1)}, u32[]{:S(2)}, u32[]{:S(2)}) collective-permute-start(f32[8,128]{1,0:T(8,128)S(1)} %quad_sum.2.own_ref), channel_id=1, source_target_pairs={{0,8},{1,9},{2,10},{3,11},{4,12},{5,13},{6,14},{7,15},{8,0},{9,1},... | collective-permute-start | bytes 12296 | tf_op jit(solution)/shard_map/ppermute | solution.py:456
  102.7 4.5 %collective-permute-start.5 = (f32[8,128]{1,0:T(8,128)S(1)}, f32[8,128]{1,0:T(8,128)S(1)}, u32[]{:S(2)}, u32[]{:S(2)}) collective-permute-start(f32[8,128]{1,0:T(8,128)S(1)} %quad_sum.2.own_ref), channel_id=1, source_target_pairs={{0,12},{1,13},{2,14},{3,15},{4,8},{5,9},{6,10},{7,11},{8,4},{9,5},... | collective-permute-start | bytes 12296 | tf_op jit(solution)/shard_map/ppermute | solution.py:456
  107.3 4.5 %collective-permute-start.6 = (f32[8,128]{1,0:T(8,128)S(1)}, f32[8,128]{1,0:T(8,128)S(1)}, u32[]{:S(2)}, u32[]{:S(2)}) collective-permute-start(f32[8,128]{1,0:T(8,128)S(1)} %quad_sum.3.own_ref), channel_id=1, source_target_pairs={{0,16},{1,17},{2,18},{3,19},{4,20},{5,21},{6,22},{7,23},{8,24},{9,... | collective-permute-start | bytes 12296 | tf_op jit(solution)/shard_map/ppermute | solution.py:456
